TPU v7x, 512 devices: a whole 4x8x8 slice. The times are simulated.
512 devices in a mesh: wide: 32 (over x, z), narrow: 16 (over y, core).
Axes of the slice: x: 4, y: 8, z: 8, core: 2. Of those that a mesh axis runs over, the one named last changes fastest.
Arguments:
- tokens: bfloat16 [1024, 256, 512], P(('wide', 'narrow')), may hold values from -6 to 6
- cotangent: bfloat16 [1024, 256, 512], P(('wide', 'narrow')), may hold values from -0.29882812 to 0.29882812
- lengths: int32 [1024], P(('wide', 'narrow')), may hold values from 160 to 256, as said below
- item_rows: int32 [1024, 256], P(('wide', 'narrow')), may hold values from 0 to 16383, as said below
- w_in: bfloat16 [512, 2048], replicated, may hold values from -0.25 to 0.25
- w_out: bfloat16 [512, 512], replicated, may hold values from -0.25 to 0.25
- table: float32 [16384, 512], P(('wide', 'narrow')), may hold values from -6 to 6
- moment_one: float32 [16384, 512], P(('wide', 'narrow')), may hold values from -0.3 to 0.3
- moment_two: float32 [16384, 512], P(('wide', 'narrow')), may hold values from 0.0001 to 0.01
Outputs:
- table_new: float32 [16384, 512], P(('wide', 'narrow'))
- moment_one_new: float32 [16384, 512], P(('wide', 'narrow'))
- moment_two_new: float32 [16384, 512], P(('wide', 'narrow'))
Inputs may be any that keep to these rules, and one draw needn't show every extreme that they name: `lengths`: some sequence has exactly 256 live positions. `item_rows`: A row r has inner block index (r // 32) % 16. In every sequence at most 32 of the 256 positions name rows of one inner block index, and some index is named by exactly 32 of them.
All inputs are finite; a program needn't handle non-finite values.
Results may differ from a plain program's by a relative error of at most 0.005.
Values may be sent and summed in bfloat16 or wider, within the bound.
A program may use at most 64 MiB of HBM per device.

v0:
```python
import jax
import jax.numpy as jnp
from jax import lax
from jax.sharding import PartitionSpec as P

HEADS = 8


norm_eps = 1e-06
clip_norm = 4.0
learn_rate = 0.5
beta_first = 0.9
beta_second = 0.999
adam_step = 3.0
adam_eps = 1e-08


def in_blocks(array, dim, devices):
    before, after = (array.shape[:dim], array.shape[dim + 1 :])
    return jnp.moveaxis(array.reshape(*before, devices, -1, *after), dim, 0)


def sum_at_owner(array, axis, dim):
    pieces = in_blocks(array, dim, lax.axis_size(axis))
    arrived = lax.all_to_all(pieces, axis, split_axis=0, concat_axis=0, tiled=True)
    return arrived.astype(jnp.float32).sum(axis=0)


def layer_forward(source, w_in, w_out, length):
    positions, width = source.shape
    per_head = width // HEADS
    inner = jnp.dot(source.astype(jnp.bfloat16), w_in, preferred_element_type=jnp.float32)
    hidden = jax.nn.silu(inner).astype(jnp.bfloat16)
    gate_part, value_part, query_part, key_part = jnp.split(hidden, 4, axis=1)
    query_part = query_part.reshape(positions, HEADS, per_head)
    key_part = key_part.reshape(positions, HEADS, per_head)
    value_part = value_part.reshape(positions, HEADS, per_head)
    scores = jnp.einsum(
        "qhd,khd->hqk", query_part, key_part, preferred_element_type=jnp.float32
    ) * per_head ** (-0.5)
    index_row = jnp.arange(positions)
    allowed = ((index_row[None, :] <= index_row[:, None]) & (index_row[:, None] < length)).astype(
        jnp.float32
    )
    attention = (jax.nn.silu(scores) * allowed[None] / length.astype(jnp.float32)).astype(
        jnp.bfloat16
    )
    mixed = jnp.einsum(
        "hqk,khd->qhd", attention, value_part, preferred_element_type=jnp.float32
    ).reshape(positions, width)
    centered = mixed - jnp.mean(mixed, axis=1, keepdims=True)
    normed = centered * lax.rsqrt(jnp.mean(centered * centered, axis=1, keepdims=True) + norm_eps)
    gated = (normed * gate_part.astype(jnp.float32)).astype(jnp.bfloat16)
    return jnp.dot(gated, w_out, preferred_element_type=jnp.float32) + source


def token_grads(inputs, cotangent, length, w_in, w_out):
    live_mask = (jnp.arange(inputs.shape[0]) < length).astype(jnp.float32)
    _, pullback = jax.vjp(
        lambda source_rows: layer_forward(source_rows, w_in, w_out, length),
        inputs.astype(jnp.float32),
    )
    (gradient,) = pullback(cotangent.astype(jnp.float32) * live_mask[:, None])
    return gradient.astype(jnp.bfloat16)


def pack_rows(gradients, row_ids, owners, rows_dev, owned):
    batch_count, slots, width = gradients.shape
    capacity = 2 * slots // owners
    blocks = row_ids // rows_dev
    owner_index = blocks % owners
    local_rows = blocks // owners * rows_dev + row_ids % rows_dev
    hits_table = (owner_index[:, :, None] == jnp.arange(owners)[None, None, :]).astype(jnp.int32)
    ranking = jnp.sum((jnp.cumsum(hits_table, axis=1) - 1) * hits_table, axis=2)
    placed = (
        owner_index * (batch_count * capacity)
        + jnp.arange(batch_count)[:, None] * capacity
        + ranking
    )
    total_slots = owners * batch_count * capacity
    outgoing = (
        jnp.zeros((total_slots, width), jnp.bfloat16)
        .at[placed.reshape(-1)]
        .set(gradients.reshape(-1, width))
    )
    labels = (
        jnp.full((total_slots,), owned, jnp.int32)
        .at[placed.reshape(-1)]
        .set(local_rows.reshape(-1))
    )
    return (
        outgoing.reshape(owners, batch_count * capacity, width),
        labels.reshape(owners, batch_count * capacity),
    )


def owner_total(arrived, arrived_labels, owned):
    row_data = arrived.reshape(-1, arrived.shape[-1])
    flat_labels = arrived_labels.reshape(-1)
    empty = jnp.zeros((owned, row_data.shape[1]), jnp.float32)
    return empty.at[flat_labels].add(row_data.astype(jnp.float32), mode="drop")


def adam_rows(row_grad, table, moment_one, moment_two):
    row_norms = jnp.sqrt(jnp.sum(row_grad * row_grad, axis=1, keepdims=True))
    clipped = row_grad * (clip_norm / jnp.maximum(row_norms, clip_norm))
    first_moment = beta_first * moment_one + (1.0 - beta_first) * clipped
    second_moment = beta_second * moment_two + (1.0 - beta_second) * clipped * clipped
    step_size = learn_rate / (1.0 - beta_first**adam_step)
    scaled = jnp.sqrt(second_moment / (1.0 - beta_second**adam_step)) + adam_eps
    return (table - step_size * first_moment / scaled, first_moment, second_moment)


def on_device(tokens, cotangent, lengths, item_rows, w_in, w_out, table, moment_one, moment_two):
    owners = lax.axis_size("narrow")
    rows_dev = table.shape[0]
    owned = lax.axis_size("wide") * rows_dev
    backward = jax.vmap(token_grads, in_axes=(0, 0, 0, None, None))
    gradients = backward(tokens, cotangent, lengths, w_in, w_out)
    outgoing, labels = pack_rows(gradients, item_rows, owners, rows_dev, owned)
    arrived, arrived_labels = (
        lax.all_to_all(outgoing, "narrow", split_axis=0, concat_axis=0, tiled=True),
        lax.all_to_all(labels, "narrow", split_axis=0, concat_axis=0, tiled=True),
    )
    row_grad = owner_total(arrived, arrived_labels, owned)
    owned_rows = sum_at_owner(row_grad.astype(jnp.bfloat16), "wide", 0)
    return adam_rows(owned_rows, table, moment_one, moment_two)


def solution(mesh):
    return jax.shard_map(
        on_device,
        mesh=mesh,
        in_specs=(
            P(("wide", "narrow"), None, None),
            P(("wide", "narrow"), None, None),
            P(("wide", "narrow")),
            P(("wide", "narrow"), None),
            P(),
            P(),
            P(("wide", "narrow"), None),
            P(("wide", "narrow"), None),
            P(("wide", "narrow"), None),
        ),
        out_specs=(
            P(("wide", "narrow"), None),
            P(("wide", "narrow"), None),
            P(("wide", "narrow"), None),
        ),
        check_vma=False,
    )
```

profile of v0, /device:TPU:1, one launch (start us, length us, event | category | flops | bytes accessed | tf_op | source)
XLA Modules:
  0.0 148.0 jit_solution(18362284450512683484)
XLA Ops:
  0.7 0.8 fusion.57
  1.6 1.2 reduce-window.6
  3.2 2.4 %scatter_custom_fusion = s32[1024]{0:T(1024)S(1)} fusion(s32[512]{0:T(512)S(1)} %bitcast.103, s32[512]{0:T(512)S(1)} %bitcast.105, s32[]{:T(128)} %constant.79.clone.1), kind=kCustom, calls=%fused_computation.89 | custom fusion | bytes 4100 | tf_op jit(solution)/shard_map/scatter | solution.py:89
  5.6 0.7 all_to_all.12
  6.3 10.1 %all-to-all-start = ((s32[16,1,64]{2,1,0:T(1,128)}), s32[16,1,64]{2,1,0:T(1,128)S(1)}, u32[]{:S(2)}, u32[]{:S(2)}) async-start(s32[16,1,64]{2,1,0:T(1,128)} %all_to_all.12), calls=%async_computation | async-start | bytes 16384 | tf_op jit(solution)/shard_map/all_to_all | solution.py:123
  16.4 0.7 fusion.61
  17.8 4.6 %multiply_convert_fusion = (bf16[2,256,2048]{2,1,0:T(8,128)(2,1)S(1)}, f32[2,256,2048]{2,1,0:T(8,128)}) fusion(bf16[2,256,512]{2,1,0:T(8,128)(2,1)} %param.9, bf16[512,2048]{1,0:T(8,128)(2,1)S(1)} %copy-done), kind=kOutput, calls=%fused_computation.15 | convolution fusion | flops 1078984704 | bytes 8912896 | tf_op jit(solution)/shard_map/vmap(jvp())/dot_general | solution.py:32
  22.4 1.4 copy-done.3
  23.8 1.1 fusion.63
  25.1 1.4 copy.35
  26.6 2.3 %copy.33 = bf16[2,256,512]{1,2,0:T(8,128)(2,1)} copy(bf16[2,256,512]{2,1,0:T(8,128)(2,1)} %get-tuple-element.8) | data formatting | bytes 1048576 | tf_op jit(solution)/shard_map/vmap(jvp())/split | solution.py:34
  29.0 3.6 %divide_convert_fusion = (bf16[2,8,256,256]{3,2,1,0:T(8,128)(2,1)S(1)}, f32[2,8,256,256]{3,2,1,0:T(8,128)}) fusion(f32[2]{0:T(128)S(1)} %convert_element_type.98, f32[2,256,256]{2,1,0:T(8,128)S(1)} %and_convert_fusion, bf16[2,256,8,64]{1,3,2,0:T(8,128)(2,1)S(1)} %bitcast.92, bf16[2,256,8,64]{1,3,2,0:T(8,128)(2,1)S(1)} %bitcast.94), kind=kOutput, calls=%fused_computation.13 | convolution fusion | flops 142606336 | bytes 7864328 | tf_op jit(solution)/shard_map/vmap(jvp(qhd,khd->hqk))/dot_general | solution.py:38
  32.6 1.3 copy-done.2
  33.9 0.8 bitcast_reduce_fusion
  34.7 1.4 copy.36
  36.2 2.4 %multiply_reduce_fusion = (f32[2,256]{1,0:T(2,128)S(1)}, bf16[2,256,512]{2,1,0:T(8,128)(2,1)S(1)}) fusion(f32[2,256,512]{2,1,0:T(8,128)} %copy.36, f32[2,256]{1,0:T(2,128)S(1)} %broadcast_multiply_fusion, bf16[2,256,2048]{2,1,0:T(8,128)(2,1)} %copy-done.3, bf16[512,512]{1,0:T(8,128)(2,1)} %param.14, bf16[2,256,512]{2,1,0:T(8,128)(2,1)} %param.10, ...), kind=kOutput, calls=%fused_computation.47 | convolution fusion | flops 270794240 | bytes 3151872 | tf_op jit(solution)/shard_map/vmap(transpose(jvp()))/dot_general | solution.py:54
  38.8 1.4 fusion.41
  40.5 1.1 copy.37
  41.6 2.2 %fusion.66 = bf16[2,8,64,256]{3,2,1,0:T(8,128)(2,1)S(1)} fusion(bf16[2,8,64,256]{3,2,1,0:T(8,128)(2,1)} %bitcast.97, bf16[2,8,256,256]{3,2,1,0:T(8,128)(2,1)} %copy-done.2), kind=kOutput, calls=%fused_computation.106 | convolution fusion | flops 134217728 | bytes 3145728 | tf_op jit(solution)/shard_map/vmap(transpose(jvp(hqk,khd->qhd)))/dot_general | solution.py:48
  43.9 4.5 %fusion.7 = bf16[2,8,256,256]{3,2,1,0:T(8,128)(2,1)S(1)} fusion(f32[2,8,256,256]{3,2,1,0:T(8,128)} %get-tuple-element.20, f32[2]{0:T(128)S(1)} %convert_element_type.98, f32[2,256,256]{2,1,0:T(8,128)} %copy-done.11, bf16[2,8,64,256]{3,2,1,0:T(8,128)(2,1)} %bitcast.98, bf16[2,256,8,64]{1,3,2,0:T(8,128)(2,1)S(1)} %bitcast.91), kind=kOutput, calls=%fused_computation.12 | convolution fusion | flops 149946368 | bytes 7864328 | tf_op jit(solution)/shard_map/vmap(transpose(jvp(hqk,khd->qhd)))/dot_general | solution.py:48
  48.4 0.7 fusion.65
  49.2 1.3 fusion.64
  50.5 1.0 copy.38
  51.7 1.3 copy.40
  52.9 5.3 %fusion.36 = bf16[2,256,512]{2,1,0:T(8,128)(2,1)} fusion(bf16[512,2048]{1,0:T(8,128)(2,1)S(1)} %copy-done, f32[2,256,2048]{2,1,0:T(8,128)} %get-tuple-element.18, bf16[2,256,512]{2,1,0:T(8,128)(2,1)S(1)} %copy.40, bf16[2,256,512]{2,1,0:T(8,128)(2,1)S(1)} %copy.39, bf16[2,256,512]{2,1,0:T(8,128)(2,1)} %copy.38, bf16[2,256,512]{2,1,0:T(8,128)(2,1)} %get-tuple-element.11, ...), kind=kOutput, calls=%fused_computation.37 | convolution fusion | flops 1093140480 | bytes 9439232 | tf_op jit(solution)/shard_map/vmap(transpose(jvp()))/dot_general | solution.py:32
  58.3 4.2 %scatter_custom_fusion.1 = bf16[1024,512]{1,0:T(8,128)(2,1)} fusion(s32[512]{0:T(512)S(1)} %bitcast.104, bf16[512,512]{1,0:T(8,128)(2,1)} %bitcast.106, bf16[]{:T(256)} %constant.90.clone.1), kind=kCustom, calls=%fused_computation.53 | custom fusion | bytes 1049088 | tf_op jit(solution)/shard_map/scatter | solution.py:84
  62.4 7.3 %all-to-all-start.1 = ((bf16[16,64,512]{2,1,0:T(8,128)(2,1)}), bf16[16,64,512]{2,1,0:T(8,128)(2,1)S(1)}, u32[]{:S(2)}, u32[]{:S(2)}) async-start(bf16[16,64,512]{2,1,0:T(8,128)(2,1)} %bitcast.20), calls=%async_computation.1 | async-start | bytes 2097152 | tf_op jit(solution)/shard_map/all_to_all | solution.py:122
  71.0 26.7 %all-to-all-done.1 = bf16[16,64,512]{2,1,0:T(8,128)(2,1)S(1)} async-done(((bf16[16,64,512]{2,1,0:T(8,128)(2,1)}), bf16[16,64,512]{2,1,0:T(8,128)(2,1)S(1)}, u32[]{:S(2)}, u32[]{:S(2)}) %all-to-all-start.1) | async-done | bytes 1048608 | tf_op jit(solution)/shard_map/all_to_all | solution.py:122
  97.7 8.2 %scatter_custom_fusion.2 = f32[1024,512]{1,0:T(8,128)} fusion(s32[1024]{0:T(1024)S(1)} %bitcast.102, bf16[1024,512]{1,0:T(8,128)(2,1)S(1)} %bitcast.89, f32[]{:T(128)} %constant.78.clone.1), kind=kCustom, calls=%fused_computation.24 | custom fusion | flops 1048576 | bytes 3145732 | tf_op jit(solution)/shard_map/scatter-add | solution.py:101
  105.9 1.7 %convert_element_type.118 = bf16[1024,512]{1,0:T(8,128)(2,1)S(1)} convert(f32[1024,512]{1,0:T(8,128)} %scatter_custom_fusion.2) | non-fusion elementwise | flops 524288 | bytes 3145728 | tf_op jit(solution)/shard_map/convert_element_type | solution.py:126
  107.6 39.3 %all_to_all.19 = bf16[32,32,512]{2,1,0:T(8,128)(2,1)S(1)} all-to-all(bf16[32,32,512]{2,1,0:T(8,128)(2,1)S(1)} %bitcast.88), channel_id=1, replica_groups=mesh['wide'=32,'narrow'=16] {'wide'}, dimensions={0} | all-to-all | bytes 2097152 | tf_op jit(solution)/shard_map/all_to_all | solution.py:25
  147.2 0.8 divide_subtract_fusion
  (58 shorter events, 3.9 us)
Async XLA Ops:
  0.6 17.2 %copy-start = (bf16[512,2048]{1,0:T(8,128)(2,1)S(1)}, bf16[512,2048]{1,0:T(8,128)(2,1)}, u32[]{:S(2)}) copy-start(bf16[512,2048]{1,0:T(8,128)(2,1)} %param.13) | copy-start | bytes 6291460
  6.3 56.1 %all-to-all-start = ((s32[16,1,64]{2,1,0:T(1,128)}), s32[16,1,64]{2,1,0:T(1,128)S(1)}, u32[]{:S(2)}, u32[]{:S(2)}) async-start(s32[16,1,64]{2,1,0:T(1,128)} %all_to_all.12), calls=%async_computation | async-start | bytes 16384 | tf_op jit(solution)/shard_map/all_to_all | solution.py:123
  22.4 1.4 copy-start.3
  25.1 7.5 %copy-start.7 = (bf16[2,256,512]{1,2,0:T(8,128)(2,1)}, bf16[2,256,512]{1,2,0:T(8,128)(2,1)S(1)}, u32[]{:S(2)}) copy-start(bf16[2,256,512]{1,2,0:T(8,128)(2,1)S(1)} %copy.34) | copy-start | bytes 1572868
  26.5 6.0 %copy-start.9 = (bf16[2,256,512]{1,2,0:T(8,128)(2,1)}, bf16[2,256,512]{1,2,0:T(8,128)(2,1)S(1)}, u32[]{:S(2)}) copy-start(bf16[2,256,512]{1,2,0:T(8,128)(2,1)S(1)} %copy.35) | copy-start | bytes 1572868
  29.0 3.6 %copy-start.11 = (f32[2,256,256]{2,1,0:T(8,128)}, f32[2,256,256]{2,1,0:T(8,128)S(1)}, u32[]{:S(2)}) copy-start(f32[2,256,256]{2,1,0:T(8,128)S(1)} %and_convert_fusion) | copy-start | bytes 1572868
  29.0 4.9 %copy-start.5 = (bf16[2,256,512]{1,2,0:T(8,128)(2,1)S(1)}, bf16[2,256,512]{1,2,0:T(8,128)(2,1)}, u32[]{:S(2)}) copy-start(bf16[2,256,512]{1,2,0:T(8,128)(2,1)} %copy.33) | copy-start | bytes 1572868
  32.6 1.3 copy-start.2
  36.1 2.6 %copy-start.1 = (f32[2,256,512]{2,1,0:T(8,128)S(1)}, f32[2,256,512]{2,1,0:T(8,128)}, u32[]{:S(2)}) copy-start(f32[2,256,512]{2,1,0:T(8,128)} %copy.36) | copy-start | bytes 3145732
  36.1 2.7 %copy-start.4 = (bf16[2,256,2048]{2,1,0:T(8,128)(2,1)S(1)}, bf16[2,256,2048]{2,1,0:T(8,128)(2,1)}, u32[]{:S(2)}) copy-start(bf16[2,256,2048]{2,1,0:T(8,128)(2,1)} %copy-done.3) | copy-start | bytes 6291460
  38.8 5.1 %copy-start.6 = (bf16[2,256,512]{1,2,0:T(8,128)(2,1)S(1)}, bf16[2,256,512]{1,2,0:T(8,128)(2,1)}, u32[]{:S(2)}) copy-start(bf16[2,256,512]{1,2,0:T(8,128)(2,1)} %copy.33) | copy-start | bytes 1572868
  43.8 4.6 %copy-start.10 = (bf16[2,256,512]{1,2,0:T(8,128)(2,1)S(1)}, bf16[2,256,512]{1,2,0:T(8,128)(2,1)}, u32[]{:S(2)}) copy-start(bf16[2,256,512]{1,2,0:T(8,128)(2,1)} %copy-done.9) | copy-start | bytes 1572868
  43.9 5.3 %copy-start.8 = (bf16[2,256,512]{1,2,0:T(8,128)(2,1)S(1)}, bf16[2,256,512]{1,2,0:T(8,128)(2,1)}, u32[]{:S(2)}) copy-start(bf16[2,256,512]{1,2,0:T(8,128)(2,1)} %copy-done.7) | copy-start | bytes 1572868
  62.4 35.3 %all-to-all-start.1 = ((bf16[16,64,512]{2,1,0:T(8,128)(2,1)}), bf16[16,64,512]{2,1,0:T(8,128)(2,1)S(1)}, u32[]{:S(2)}, u32[]{:S(2)}) async-start(bf16[16,64,512]{2,1,0:T(8,128)(2,1)} %bitcast.20), calls=%async_computation.1 | async-start | bytes 2097152 | tf_op jit(solution)/shard_map/all_to_all | solution.py:122
  97.7 49.5 %copy-start.12 = (f32[32,512]{1,0:T(8,128)S(1)}, f32[32,512]{1,0:T(8,128)}, u32[]{:S(2)}) copy-start(f32[32,512]{1,0:T(8,128)} %param.15) | copy-start | bytes 196612
  97.7 49.5 %copy-start.13 = (f32[32,512]{1,0:T(8,128)S(1)}, f32[32,512]{1,0:T(8,128)}, u32[]{:S(2)}) copy-start(f32[32,512]{1,0:T(8,128)} %param.16) | copy-start | bytes 196612
  97.7 49.5 %copy-start.14 = (f32[32,512]{1,0:T(8,128)S(1)}, f32[32,512]{1,0:T(8,128)}, u32[]{:S(2)}) copy-start(f32[32,512]{1,0:T(8,128)} %param.17) | copy-start | bytes 196612
where the time goes:
time: 149 us; the launch traced here: 148 us
  blocking collectives  39.3 us (26%)
  waiting for transfers between devices  26.7 us (18%)
  matrix products  25.5 us (17%)
  local copies, waits for them, and re-layouts  20.9 us (14%)
  starting transfers between devices  17.4 us (12%)
  other arithmetic  17.3 us (12%)
    all_to_all x1, blocking collectives, sum_at_owner(): lax.all_to_all(pieces, axis, split_axis=0, concat_axis=0, tiled=True)  39.3 us
    all_to_all x1, waiting for transfers between devices, on_device(): lax.all_to_all(outgoing, 'narrow', split_axis=0, concat_axis=0, tiled=True)  26.7 us
    all_to_all x1, starting transfers between devices, on_device(): lax.all_to_all(labels, 'narrow', split_axis=0, concat_axis=0, tiled=True)  10.1 us
    dot_general x2, matrix products, layer_forward(): jnp.dot(source.astype(jnp.bfloat16), w_in, preferred_element_type=jnp.flo...  9.9 us
    scatter-add x1, other arithmetic, owner_total(): return empty.at[flat_labels].add(row_data.astype(jnp.float32), mode='drop')  8.15 us
    dot_general x3, matrix products, layer_forward(): jnp.einsum('hqk,khd->qhd', attention, value_part, preferred_element_type=...  7.55 us
    all_to_all x1, starting transfers between devices, on_device(): lax.all_to_all(outgoing, 'narrow', split_axis=0, concat_axis=0, tiled=True)  7.27 us
    dot_general x3, matrix products, layer_forward(): jnp.einsum('qhd,khd->hqk', query_part, key_part, preferred_element_type=j...  5.65 us
  transfers between devices with their start and end apart: 2, of which 1 were waited for; matrix products, arithmetic and copies ran while one was open for 30% of the time, Pallas kernels for 0%

commit v1 on v0

v1 whole, which is shorter than its diff:
```python
import functools

import jax
import jax.numpy as jnp
from jax import lax
from jax.experimental import pallas as pl
from jax.experimental.pallas import tpu as pltpu
from jax.sharding import PartitionSpec as P

HEADS = 8
BF = jnp.bfloat16
F32 = jnp.float32
I32 = jnp.int32
MESH = pl.DeviceIdType.MESH
CW = 128
X_CHIPS = 4

norm_eps = 1e-06
clip_norm = 4.0
learn_rate = 0.5
beta_first = 0.9
beta_second = 0.999
adam_step = 3.0
adam_eps = 1e-08


def nn(a, b):
    return lax.dot_general(a, b, (((1,), (0,)), ((), ())), preferred_element_type=F32)


def nt(a, b):
    return lax.dot_general(a, b, (((1,), (1,)), ((), ())), preferred_element_type=F32)


def adam_rows(row_grad, table, moment_one, moment_two):
    row_norms = jnp.sqrt(jnp.sum(row_grad * row_grad, axis=1, keepdims=True))
    clipped = row_grad * (clip_norm / jnp.maximum(row_norms, clip_norm))
    first_moment = beta_first * moment_one + (1.0 - beta_first) * clipped
    second_moment = beta_second * moment_two + (1.0 - beta_second) * clipped * clipped
    step_size = learn_rate / (1.0 - beta_first**adam_step)
    scaled = jnp.sqrt(second_moment / (1.0 - beta_second**adam_step)) + adam_eps
    return (table - step_size * first_moment / scaled, first_moment, second_moment)


def iota(shape, dim):
    return lax.broadcasted_iota(I32, shape, dim)


def as_one(flags):
    return jnp.where(flags, 1.0, 0.0).astype(BF)


def layout_rows(s, items, owners, cap, rows_dev, pack, lab_send):
    positions = items.shape[1]
    ids = items[pl.ds(s, 1), :]
    ids_col = jnp.transpose(jnp.broadcast_to(ids.astype(F32), (8, positions)))[:, 0:1].astype(I32)
    owner = (ids // rows_dev) % owners
    owner_col = (ids_col // rows_dev) % owners
    before = (owner_col == owner) & (iota((positions, positions), 0) < iota((positions, positions), 1))
    rank = jnp.sum(jnp.where(before, 1.0, 0.0), axis=0, keepdims=True)
    rank_col = jnp.transpose(jnp.broadcast_to(rank, (8, positions)))[:, 0:1].astype(I32)
    slot = owner * cap + rank.astype(I32)
    pack[s] = as_one(iota((owners * cap, positions), 0) == slot)
    ranks = as_one(iota((positions, 128), 1) % cap == rank_col)
    mine = iota((owners, positions), 0) == owner
    high = jnp.where(mine, (ids // (rows_dev * owners) + 1).astype(F32), 0.0).astype(BF)
    low = jnp.where(mine, (ids % rows_dev).astype(F32), 0.0).astype(BF)
    labels = (nn(high, ranks) - 1.0) * float(rows_dev) + nn(low, ranks)
    for d in range(owners):
        lab_send[d, pl.ds(s, 1), :] = labels[d : d + 1, :]


def sequence_grad(s, tokens, cot, lengths, w_in, w_out, hid, der, att, fac, mixed, ds, dmx, dinner, wmask):
    positions, width = tokens.shape[1:]
    half = positions // 2
    per_head = width // HEADS
    x = tokens[s]
    n = lengths[s]
    for part in range(4):
        cols = slice(part * width, (part + 1) * width)
        inner = nn(x, w_in[:, cols])
        sig = 0.5 * jnp.tanh(0.5 * inner) + 0.5
        act = inner * sig
        hid[:, cols] = act.astype(BF)
        der[:, cols] = sig + act * (1.0 - sig)
    pos = iota((positions, 1), 0)
    live = jnp.where(pos < n, 1.0, 0.0)
    weight = live / jnp.full((positions, 1), n, I32).astype(F32)
    causal = iota((half, half), 1) <= iota((half, half), 0)
    wmask[0] = jnp.where(causal, weight[:half], 0.0)
    wmask[1] = jnp.broadcast_to(weight[half:], (half, half))
    wmask[2] = jnp.where(causal, weight[half:], 0.0)
    low = iota((positions, 128), 1) < per_head
    ones = (jnp.where(iota((1, 128), 1) < per_head, 1.0, 0.0).astype(BF), jnp.where(iota((1, 128), 1) < per_head, 0.0, 1.0).astype(BF))
    scale = per_head ** (-0.5)

    def score(block, wm):
        sig = 0.5 * jnp.tanh(0.5 * block) + 0.5
        act = block * sig
        return (act * wm).astype(BF), (sig + act * (1.0 - sig)) * wm

    for pair in range(HEADS // 2):
        v2 = hid[:, width + pair * 128 : width + (pair + 1) * 128]
        q2 = hid[:, 2 * width + pair * 128 : 2 * width + (pair + 1) * 128]
        k2 = hid[:, 3 * width + pair * 128 : 3 * width + (pair + 1) * 128]
        for h in range(2):
            head = 2 * pair + h
            qm = q2 * (ones[h] * scale)
            a, f = score(nt(qm[:half], k2[:half]), wmask[0])
            att[head, :half, :half] = a
            fac[head, :half, :half] = f
            below = nt(qm[half:], k2)
            a, f = score(below[:, :half], wmask[1])
            att[head, half:, :half] = a
            fac[head, half:, :half] = f
            a, f = score(below[:, half:], wmask[2])
            att[head, half:, half:] = a
            fac[head, half:, half:] = f
        mixed[:, pair * 128 : (pair + 1) * 128] = jnp.where(low, nn(att[2 * pair], v2), nn(att[2 * pair + 1], v2))

    mix = mixed[...]
    centered = mix - jnp.mean(mix, axis=1, keepdims=True)
    inv = lax.rsqrt(jnp.mean(centered * centered, axis=1, keepdims=True) + norm_eps)
    normed = centered * inv
    dgated = (nt(cot[s], w_out[...]) * live).astype(BF).astype(F32)
    gate = hid[:, :width].astype(F32)
    dgate = (dgated * normed).astype(BF).astype(F32)
    dinner[:, :width] = (dgate * der[:, :width]).astype(BF)
    dnormed = dgated * gate
    dcentered = inv * (dnormed - normed * jnp.mean(dnormed * normed, axis=1, keepdims=True))
    dmx[...] = (dcentered - jnp.mean(dcentered, axis=1, keepdims=True)).astype(BF)

    for pair in range(HEADS // 2):
        lanes = slice(pair * 128, (pair + 1) * 128)
        v_at = slice(width + pair * 128, width + (pair + 1) * 128)
        q_at = slice(2 * width + pair * 128, 2 * width + (pair + 1) * 128)
        k_at = slice(3 * width + pair * 128, 3 * width + (pair + 1) * 128)
        v2, k2 = hid[:, v_at], hid[:, k_at]
        dm2 = dmx[:, lanes]
        dm2_t = jnp.transpose(dm2)
        q2_t = jnp.transpose(hid[:, q_at])
        for h in range(2):
            head = 2 * pair + h
            dmm = dm2 * ones[h]
            d = nt(dmm[:half], v2[:half])
            ds[h, :half, :half] = (d.astype(BF).astype(F32) * fac[head, :half, :half]).astype(BF)
            d = nt(dmm[half:], v2)
            ds[h, half:, :] = (d.astype(BF).astype(F32) * fac[head, half:, :]).astype(BF)
        dv = jnp.concatenate([nn(dm2_t[:per_head], att[2 * pair]), nn(dm2_t[per_head:], att[2 * pair + 1])], axis=0)
        dk = jnp.concatenate([nn(q2_t[:per_head], ds[0]), nn(q2_t[per_head:], ds[1])], axis=0)
        dq = jnp.where(low, nn(ds[0], k2), nn(ds[1], k2))
        dinner[:, v_at] = (jnp.transpose(dv).astype(BF).astype(F32) * der[:, v_at]).astype(BF)
        dinner[:, q_at] = ((dq * scale).astype(BF).astype(F32) * der[:, q_at]).astype(BF)
        dinner[:, k_at] = ((jnp.transpose(dk) * scale).astype(BF).astype(F32) * der[:, k_at]).astype(BF)
    return live


def kernel(
    dims, tokens, cot, lengths, items, w_in, w_out, out,
    hid, der, att, fac, mixed, ds, dmx, dinner, wmask, pack, lab_send, lab_recv, onehot,
    send_y, recv_y, acc, send_x, recv_x, own_z, send_z, recv_z,
    sem_lab, sem_y_send, sem_y_recv, sem_x_send, sem_x_recv, sem_z_send, sem_z_recv,
):
    nx, nz, ny, cores, rows_dev = dims
    micro, positions, width = tokens.shape
    owners = ny * cores
    cap = 2 * positions // owners
    slots = owners * cap
    owned = nx * nz * rows_dev
    x_rows = nz * rows_dev
    chunks = width // CW
    wide, narrow = lax.axis_index("wide"), lax.axis_index("narrow")
    my_x, my_z = wide // nz, wide % nz
    my_y, my_core = narrow // cores, narrow % cores

    hops = sorted(((dy, dc) for dy in range(ny) for dc in range(cores)), key=lambda h: (-min(h[0], ny - h[0]), h[1], h[0]))
    hops.remove((0, 0))
    near = [((my_y + dy) % ny) * cores + (my_core + dc) % cores for dy, dc in hops]
    x_peers = [(my_x + d) % nx for d in range(1, nx)]
    z_peers = [(my_z + d) % nz for d in range(1, nz)]

    barrier = pltpu.get_barrier_semaphore()
    for peer in near:
        pl.semaphore_signal(barrier, inc=1, device_id=(wide, peer), device_id_type=MESH)
    for peer in x_peers:
        pl.semaphore_signal(barrier, inc=1, device_id=(peer * nz + my_z, narrow), device_id_type=MESH)
    for peer in z_peers:
        pl.semaphore_signal(barrier, inc=1, device_id=(my_x * nz + peer, narrow), device_id_type=MESH)

    half = positions // 2
    for head in range(HEADS):
        att[head, :half, half:] = jnp.zeros((half, half), BF)
    for h in range(2):
        ds[h, :half, half:] = jnp.zeros((half, half), BF)

    lab_send[...] = jnp.zeros(lab_send.shape, F32)
    for s in range(micro):
        layout_rows(s, items, owners, cap, rows_dev, pack, lab_send)
    lab_recv[0] = lab_send[narrow]

    def one_sequence(s, carry):
        live = sequence_grad(s, tokens, cot, lengths, w_in, w_out, hid, der, att, fac, mixed, ds, dmx, dinner, wmask)

        @pl.when(s == 0)
        def _():
            pl.semaphore_wait(barrier, len(near) + len(x_peers) + len(z_peers))
            for k, peer in enumerate(near):
                pltpu.make_async_remote_copy(
                    lab_send.at[peer], lab_recv.at[k + 1], sem_lab.at[0], sem_lab.at[1],
                    device_id=(wide, peer), device_id_type=MESH,
                ).start()

        for w in range(width // 256):
            cols = slice(w * 256, (w + 1) * 256)
            dx = nt(dinner[...], w_in[cols, :]).astype(BF).astype(F32)
            grad = (dx + cot[s, :, cols].astype(F32) * live).astype(BF)
            packed = nn(pack[s], grad).astype(BF)
            for c in range(w * 256 // CW, (w + 1) * 256 // CW):
                send_y[s, c] = packed[:, c * CW - w * 256 : (c + 1) * CW - w * 256]
                for k, peer in enumerate(near):
                    pltpu.make_async_remote_copy(
                        send_y.at[s, c, pl.ds(pl.multiple_of(peer * cap, cap), cap)],
                        recv_y.at[s, c, pl.ds((k + 1) * cap, cap)],
                        sem_y_send.at[s, c], sem_y_recv.at[s, c],
                        device_id=(wide, peer), device_id_type=MESH,
                    ).start()
                recv_y[s, c, :cap] = send_y[s, c, pl.ds(pl.multiple_of(narrow * cap, cap), cap), :]
        return carry

    lax.fori_loop(0, micro, one_sequence, 0)

    def whole(src, dst, send, recv):
        return pltpu.make_async_remote_copy(src, dst, send, recv, device_id=(wide, narrow), device_id_type=MESH)

    labels_in = whole(lab_send.at[pl.ds(1, owners - 1)], lab_recv.at[pl.ds(1, owners - 1)], sem_lab.at[0], sem_lab.at[1])
    labels_in.wait_recv()
    group = 128 // cap
    lane = iota((1, 128), 1)
    for s in range(micro):
        for g in range(slots // 128):
            row = lab_recv[g * group, s : s + 1, :]
            for k in range(1, group):
                row = jnp.where(lane >= k * cap, lab_recv[g * group + k, s : s + 1, :], row)
            onehot[s, :, g * 128 : (g + 1) * 128] = as_one(iota((owned, 128), 0) == row.astype(I32))

    def y_copy(s, c):
        return whole(send_y.at[s, c, pl.ds(cap, slots - cap)], recv_y.at[s, c, pl.ds(cap, slots - cap)], sem_y_send.at[s, c], sem_y_recv.at[s, c])

    def x_copy(c, d):
        peer = x_peers[d]
        return pltpu.make_async_remote_copy(
            send_x.at[c, pl.ds(pl.multiple_of(peer * x_rows, x_rows), x_rows)], recv_x.at[c, d],
            sem_x_send.at[c, d], sem_x_recv.at[c, d],
            device_id=(peer * nz + my_z, narrow), device_id_type=MESH,
        )

    def z_copy(c, d):
        peer = z_peers[d]
        return pltpu.make_async_remote_copy(
            send_z.at[c, pl.ds(pl.multiple_of(peer * rows_dev, rows_dev), rows_dev)], recv_z.at[c, d],
            sem_z_send.at[c, d], sem_z_recv.at[c, d],
            device_id=(my_x * nz + peer, narrow), device_id_type=MESH,
        )

    def owner_sum(c):
        y_copy(micro - 1, c).wait_recv()
        acc[c] += nn(onehot[micro - 1], recv_y[micro - 1, c])
        send_x[c] = acc[c].astype(BF)
        for d in range(nx - 1):
            x_copy(c, d).start()

    def x_sum(c):
        total = acc[c, pl.ds(pl.multiple_of(my_x * x_rows, x_rows), x_rows), :]
        for d in range(nx - 1):
            x_copy(c, d).wait_recv()
            total += recv_x[c, d].astype(F32)
        own_z[c] = total
        send_z[c] = total.astype(BF)
        for d in range(nz - 1):
            z_copy(c, d).start()

    def z_sum(c):
        total = own_z[c, pl.ds(pl.multiple_of(my_z * rows_dev, rows_dev), rows_dev), :]
        for d in range(nz - 1):
            z_copy(c, d).wait_recv()
            total += recv_z[c, d].astype(F32)
        out[:, c * CW : (c + 1) * CW] = total

    for c in range(chunks):
        for s in range(micro - 1):
            y_copy(s, c).wait_recv()
            part = nn(onehot[s], recv_y[s, c])
            acc[c] = part if s == 0 else acc[c] + part
    for c in range(chunks):
        owner_sum(c)
        if c >= 1:
            x_sum(c - 1)
    x_sum(chunks - 1)
    for c in range(chunks):
        z_sum(c)
    labels_in.wait_send()
    for c in range(chunks):
        for s in range(micro):
            y_copy(s, c).wait_send()
        for d in range(nx - 1):
            x_copy(c, d).wait_send()
        for d in range(nz - 1):
            z_copy(c, d).wait_send()


def on_device(dims, tokens, cotangent, lengths, item_rows, w_in, w_out, table, moment_one, moment_two):
    nx, nz, ny, cores, rows_dev = dims
    micro, positions, width = tokens.shape
    owners = ny * cores
    cap = 2 * positions // owners
    slots = owners * cap
    owned = nx * nz * rows_dev
    x_rows = nz * rows_dev
    chunks = width // CW
    vmem = pl.BlockSpec(memory_space=pltpu.VMEM)
    dma = pltpu.SemaphoreType.DMA
    row_grad = pl.pallas_call(
        functools.partial(kernel, dims),
        out_shape=jax.ShapeDtypeStruct((rows_dev, width), F32),
        in_specs=[vmem, vmem, pl.BlockSpec(memory_space=pltpu.SMEM), vmem, vmem, vmem],
        out_specs=vmem,
        scratch_shapes=[
            pltpu.VMEM((positions, 4 * width), BF),
            pltpu.VMEM((positions, 4 * width), F32),
            pltpu.VMEM((HEADS, positions, positions), BF),
            pltpu.VMEM((HEADS, positions, positions), F32),
            pltpu.VMEM((positions, width), F32),
            pltpu.VMEM((2, positions, positions), BF),
            pltpu.VMEM((positions, width), BF),
            pltpu.VMEM((positions, 4 * width), BF),
            pltpu.VMEM((3, positions // 2, positions // 2), F32),
            pltpu.VMEM((micro, slots, positions), BF),
            pltpu.VMEM((owners, 8, 128), F32),
            pltpu.VMEM((owners, 8, 128), F32),
            pltpu.VMEM((micro, owned, slots), BF),
            pltpu.VMEM((micro, chunks, slots, CW), BF),
            pltpu.VMEM((micro, chunks, slots, CW), BF),
            pltpu.VMEM((chunks, owned, CW), F32),
            pltpu.VMEM((chunks, owned, CW), BF),
            pltpu.VMEM((chunks, nx - 1, x_rows, CW), BF),
            pltpu.VMEM((chunks, x_rows, CW), F32),
            pltpu.VMEM((chunks, x_rows, CW), BF),
            pltpu.VMEM((chunks, nz - 1, rows_dev, CW), BF),
            dma((2,)),
            dma((micro, chunks)),
            dma((micro, chunks)),
            dma((chunks, nx - 1)),
            dma((chunks, nx - 1)),
            dma((chunks, nz - 1)),
            dma((chunks, nz - 1)),
        ],
        compiler_params=pltpu.CompilerParams(collective_id=0, has_side_effects=True, vmem_limit_bytes=56 * 1024 * 1024),
        name="layer_rows",
    )(tokens, cotangent, lengths, item_rows, w_in, w_out)
    return adam_rows(row_grad, table, moment_one, moment_two)


def solution(mesh, x_chips=X_CHIPS, cores=2, rows_dev=32):
    nx = x_chips
    nz = mesh.shape["wide"] // nx
    ny = mesh.shape["narrow"] // cores
    split = P(("wide", "narrow"))
    rows = P(("wide", "narrow"), None)
    return jax.shard_map(
        functools.partial(on_device, (nx, nz, ny, cores, rows_dev)),
        mesh=mesh,
        in_specs=(P(("wide", "narrow"), None, None), P(("wide", "narrow"), None, None), split, rows, P(), P(), rows, rows, rows),
        out_specs=(rows, rows, rows),
        check_vma=False,
    )
```

time: 149 us -> 60.8 us (0.41)
  Pallas kernels: 0 us -> 57.3 us
  blocking collectives: 39.3 us -> 0 us
  waiting for transfers between devices: 26.7 us -> 0 us
  matrix products: 25.5 us -> 0 us
  local copies, waits for them, and re-layouts: 20.9 us -> 0.01 us
  starting transfers between devices: 17.4 us -> 0 us
  other arithmetic: 17.3 us -> 2.58 us
    pallas_call x0 -> x1, Pallas kernels: none -> 57.3 us  [on_device(): pl.pallas_call(functools.partial(kernel, dims), out_shape=jax.ShapeDtypeS...]
    all_to_all x1 -> x0, blocking collectives: 39.3 us -> none  [sum_at_owner(): lax.all_to_all(pieces, axis, split_axis=0, concat_axis=0, tiled=True)]
    all_to_all x2 -> x0, waiting for transfers between devices: 26.7 us -> none  [the longest x1 26.7 us: on_device(): lax.all_to_all(outgoing, 'narrow', split_axis=0, concat_axis=0, tiled=True)]
    dot_general x9 -> x0, matrix products: 25.5 us -> none  [the longest x2 9.9 us: layer_forward(): jnp.dot(source.astype(jnp.bfloat16), w_in, preferred_element_type=jnp.flo...]
    all_to_all x2 -> x0, starting transfers between devices: 17.4 us -> none  [the longest x1 10.1 us: on_device(): lax.all_to_all(labels, 'narrow', split_axis=0, concat_axis=0, tiled=True)]
    scatter-add x1 -> x0, other arithmetic: 8.15 us -> none  [owner_total(): return empty.at[flat_labels].add(row_data.astype(jnp.float32), mode='drop')]
    scatter x2 -> x0, local copies, waits for them, and re-layouts: 6.6 us -> none  [the longest x1 4.15 us: pack_rows(): outgoing = jnp.zeros((total_slots, width), jnp.bfloat16).at[placed.reshap...]
    split x4 -> x0, local copies, waits for them, and re-layouts: 5.01 us -> none  [layer_forward(): gate_part, value_part, query_part, key_part = jnp.split(hidden, 4, axis=1)]
  transfers between devices with their start and end apart: 2 -> 0, of which waited for: 1 -> 0; matrix products, arithmetic and copies ran while one was open for 30% -> 0% of each run, Pallas kernels for 0% -> 0%
where the time goes in v1:
time: 60.8 us; the launch traced here: 60.5 us
  Pallas kernels  57.3 us (94%)
  other arithmetic  2.58 us (4%)
  between operations  0.69 us (1%)
    pallas_call x1, Pallas kernels, on_device(): pl.pallas_call(functools.partial(kernel, dims), out_shape=jax.ShapeDtypeS...  57.3 us
    sub x1, other arithmetic, adam_rows(): table - step_size * first_moment / scaled  1.61 us

profile of v1, /device:TPU:1, one launch (start us, length us, event | category | flops | bytes accessed | tf_op | source)
XLA Modules:
  0.0 60.5 jit_solution(11192308680056174856)
XLA Ops:
  0.6 0.0 copy-start.2
  0.6 0.0 copy-start.1
  0.7 0.0 copy-start
  0.7 57.3 %layer_rows.1 = f32[32,512]{1,0:T(8,128)} custom-call(bf16[2,256,512]{2,1,0:T(8,128)(2,1)} %tokens.1, bf16[2,256,512]{2,1,0:T(8,128)(2,1)} %cot.1, s32[2]{0:T(128)} %lengths.1, s32[2,256]{1,0:T(2,128)} %items.1, bf16[512,2048]{1,0:T(8,128)(2,1)} %w_in.1, bf16[512,512]{1,0:T(8,128)(2,1)} %w_out.1), custom_call_target="tpu_custom_call" | custom-call | tf_op jit(solution)/shard_map/layer_rows/pallas_call | solution.py:322
  57.9 1.0 %multiply_reduce_fusion = f32[32]{0:T(128)S(1)} fusion(f32[32,512]{1,0:T(8,128)} %layer_rows.1), kind=kLoop, calls=%fused_computation.4 | loop fusion | flops 32736 | bytes 65664 | tf_op jit(solution)/shard_map/reduce_sum | solution.py:36
  58.9 0.0 copy-done.2
  58.9 0.0 copy-done.1
  58.9 0.0 copy-done
  58.9 1.6 %divide_subtract_fusion = (f32[32,512]{1,0:T(8,128)}, f32[32,512]{1,0:T(8,128)}, f32[32,512]{1,0:T(8,128)}) fusion(f32[32,512]{1,0:T(8,128)S(1)} %copy-done, f32[32,512]{1,0:T(8,128)} %layer_rows.1, f32[32]{0:T(128)S(1)} %maximum_divide_fusion, f32[32,512]{1,0:T(8,128)S(1)} %copy-done.1, f32[32,512]{1,0:T(8,128)S(1)} %copy-done.2), kind=kLoop, calls=%fused_computation.2 | loop fusion | flops 212992 | bytes 458880 | tf_op jit(solution)/shard_map/sub | solution.py:42
  (1 shorter events, 0.0 us)
Async XLA Ops:
  0.6 58.3 %copy-start.2 = (f32[32,512]{1,0:T(8,128)S(1)}, f32[32,512]{1,0:T(8,128)}, u32[]{:S(2)}) copy-start(f32[32,512]{1,0:T(8,128)} %param.17) | copy-start | bytes 196612
  0.6 58.3 %copy-start.1 = (f32[32,512]{1,0:T(8,128)S(1)}, f32[32,512]{1,0:T(8,128)}, u32[]{:S(2)}) copy-start(f32[32,512]{1,0:T(8,128)} %param.16) | copy-start | bytes 196612
  0.7 58.3 %copy-start = (f32[32,512]{1,0:T(8,128)S(1)}, f32[32,512]{1,0:T(8,128)}, u32[]{:S(2)}) copy-start(f32[32,512]{1,0:T(8,128)} %param.15) | copy-start | bytes 196612

commit v2 on v1

--- a/solution.py
+++ b/solution.py
@@ -32,9 +32,11 @@
     return lax.dot_general(a, b, (((1,), (1,)), ((), ())), preferred_element_type=F32)
 
 
-def adam_rows(row_grad, table, moment_one, moment_two):
-    row_norms = jnp.sqrt(jnp.sum(row_grad * row_grad, axis=1, keepdims=True))
-    clipped = row_grad * (clip_norm / jnp.maximum(row_norms, clip_norm))
+def bits(n):
+    return n.bit_length() - 1
+
+
+def adam_rows(clipped, table, moment_one, moment_two):
     first_moment = beta_first * moment_one + (1.0 - beta_first) * clipped
     second_moment = beta_second * moment_two + (1.0 - beta_second) * clipped * clipped
     step_size = learn_rate / (1.0 - beta_first**adam_step)
@@ -54,30 +56,32 @@
     positions = items.shape[1]
     ids = items[pl.ds(s, 1), :]
     ids_col = jnp.transpose(jnp.broadcast_to(ids.astype(F32), (8, positions)))[:, 0:1].astype(I32)
-    owner = (ids // rows_dev) % owners
-    owner_col = (ids_col // rows_dev) % owners
+    owner = (ids >> bits(rows_dev)) & (owners - 1)
+    owner_col = (ids_col >> bits(rows_dev)) & (owners - 1)
     before = (owner_col == owner) & (iota((positions, positions), 0) < iota((positions, positions), 1))
     rank = jnp.sum(jnp.where(before, 1.0, 0.0), axis=0, keepdims=True)
     rank_col = jnp.transpose(jnp.broadcast_to(rank, (8, positions)))[:, 0:1].astype(I32)
     slot = owner * cap + rank.astype(I32)
     pack[s] = as_one(iota((owners * cap, positions), 0) == slot)
-    ranks = as_one(iota((positions, 128), 1) % cap == rank_col)
+    ranks = as_one((iota((positions, 128), 1) & (cap - 1)) == rank_col)
     mine = iota((owners, positions), 0) == owner
-    high = jnp.where(mine, (ids // (rows_dev * owners) + 1).astype(F32), 0.0).astype(BF)
-    low = jnp.where(mine, (ids % rows_dev).astype(F32), 0.0).astype(BF)
+    high = jnp.where(mine, ((ids >> bits(rows_dev * owners)) + 1).astype(F32), 0.0).astype(BF)
+    low = jnp.where(mine, (ids & (rows_dev - 1)).astype(F32), 0.0).astype(BF)
     labels = (nn(high, ranks) - 1.0) * float(rows_dev) + nn(low, ranks)
     for d in range(owners):
         lab_send[d, pl.ds(s, 1), :] = labels[d : d + 1, :]
 
 
-def sequence_grad(s, tokens, cot, lengths, w_in, w_out, hid, der, att, fac, mixed, ds, dmx, dinner, wmask):
+def sequence_grad(s, tokens, cot, lengths, w_in, w_out, arrived, hid, der, att, fac, mixed, ds, dmx, dinner, wmask):
     positions, width = tokens.shape[1:]
     half = positions // 2
     per_head = width // HEADS
+    arrived("tokens", s)
     x = tokens[s]
     n = lengths[s]
     for part in range(4):
         cols = slice(part * width, (part + 1) * width)
+        arrived("w_in", s, part)
         inner = nn(x, w_in[:, cols])
         sig = 0.5 * jnp.tanh(0.5 * inner) + 0.5
         act = inner * sig
@@ -122,6 +126,7 @@
     centered = mix - jnp.mean(mix, axis=1, keepdims=True)
     inv = lax.rsqrt(jnp.mean(centered * centered, axis=1, keepdims=True) + norm_eps)
     normed = centered * inv
+    arrived("cot", s)
     dgated = (nt(cot[s], w_out[...]) * live).astype(BF).astype(F32)
     gate = hid[:, :width].astype(F32)
     dgate = (dgated * normed).astype(BF).astype(F32)
@@ -156,10 +161,11 @@
 
 
 def kernel(
-    dims, tokens, cot, lengths, items, w_in, w_out, out,
+    dims, tokens_hbm, cot_hbm, lengths, items_hbm, w_in_hbm, w_out_hbm, out,
+    tokens, cot, items, w_in, w_out,
     hid, der, att, fac, mixed, ds, dmx, dinner, wmask, pack, lab_send, lab_recv, onehot,
     send_y, recv_y, acc, send_x, recv_x, own_z, send_z, recv_z,
-    sem_lab, sem_y_send, sem_y_recv, sem_x_send, sem_x_recv, sem_z_send, sem_z_recv,
+    sem_in, sem_lab, sem_y_send, sem_y_recv, sem_x_send, sem_x_recv, sem_z_send, sem_z_recv,
 ):
     nx, nz, ny, cores, rows_dev = dims
     micro, positions, width = tokens.shape
@@ -170,14 +176,38 @@
     x_rows = nz * rows_dev
     chunks = width // CW
     wide, narrow = lax.axis_index("wide"), lax.axis_index("narrow")
-    my_x, my_z = wide // nz, wide % nz
-    my_y, my_core = narrow // cores, narrow % cores
+    my_x, my_z = wide >> bits(nz), wide & (nz - 1)
+    my_y, my_core = narrow >> bits(cores), narrow & (cores - 1)
+
+    copies = {("items",): pltpu.make_async_copy(items_hbm, items, sem_in.at[0])}
+    copies["tokens", 0] = pltpu.make_async_copy(tokens_hbm.at[0], tokens.at[0], sem_in.at[1])
+    for part in range(4):
+        cols = pl.ds(part * width, width)
+        copies["w_in", part] = pltpu.make_async_copy(w_in_hbm.at[:, cols], w_in.at[:, cols], sem_in.at[2 + part])
+    copies["w_out",] = pltpu.make_async_copy(w_out_hbm, w_out, sem_in.at[6])
+    copies["cot", 0] = pltpu.make_async_copy(cot_hbm.at[0], cot.at[0], sem_in.at[7])
+    for s in range(1, micro):
+        copies["tokens", s] = pltpu.make_async_copy(tokens_hbm.at[s], tokens.at[s], sem_in.at[6 + 2 * s])
+        copies["cot", s] = pltpu.make_async_copy(cot_hbm.at[s], cot.at[s], sem_in.at[7 + 2 * s])
+    for copy in copies.values():
+        copy.start()
+
+    def arrived(name, s, part=0):
+        @pl.when(s == 0)
+        def _():
+            copies[(name, part)].wait()
+            if name == "cot":
+                copies["w_out",].wait()
+
+        if name != "w_in":
+            for later in range(1, micro):
+                pl.when(s == later)(copies[name, later].wait)
 
     hops = sorted(((dy, dc) for dy in range(ny) for dc in range(cores)), key=lambda h: (-min(h[0], ny - h[0]), h[1], h[0]))
     hops.remove((0, 0))
-    near = [((my_y + dy) % ny) * cores + (my_core + dc) % cores for dy, dc in hops]
-    x_peers = [(my_x + d) % nx for d in range(1, nx)]
-    z_peers = [(my_z + d) % nz for d in range(1, nz)]
+    near = [((my_y + dy) & (ny - 1)) * cores + ((my_core + dc) & (cores - 1)) for dy, dc in hops]
+    x_peers = [(my_x + d) & (nx - 1) for d in range(1, nx)]
+    z_peers = [(my_z + d) & (nz - 1) for d in range(1, nz)]
 
     barrier = pltpu.get_barrier_semaphore()
     for peer in near:
@@ -194,12 +224,13 @@
         ds[h, :half, half:] = jnp.zeros((half, half), BF)
 
     lab_send[...] = jnp.zeros(lab_send.shape, F32)
+    copies["items",].wait()
     for s in range(micro):
         layout_rows(s, items, owners, cap, rows_dev, pack, lab_send)
     lab_recv[0] = lab_send[narrow]
 
     def one_sequence(s, carry):
-        live = sequence_grad(s, tokens, cot, lengths, w_in, w_out, hid, der, att, fac, mixed, ds, dmx, dinner, wmask)
+        live = sequence_grad(s, tokens, cot, lengths, w_in, w_out, arrived, hid, der, att, fac, mixed, ds, dmx, dinner, wmask)
 
         @pl.when(s == 0)
         def _():
@@ -236,7 +267,8 @@
     labels_in.wait_recv()
     group = 128 // cap
     lane = iota((1, 128), 1)
-    for s in range(micro):
+
+    def owner_rows(s):
         for g in range(slots // 128):
             row = lab_recv[g * group, s : s + 1, :]
             for k in range(1, group):
@@ -285,19 +317,24 @@
             z_copy(c, d).wait_recv()
             total += recv_z[c, d].astype(F32)
         out[:, c * CW : (c + 1) * CW] = total
-
-    for c in range(chunks):
-        for s in range(micro - 1):
+        return jnp.sum(total * total, axis=1, keepdims=True)
+
+    for s in range(micro - 1):
+        owner_rows(s)
+        for c in range(chunks):
             y_copy(s, c).wait_recv()
             part = nn(onehot[s], recv_y[s, c])
             acc[c] = part if s == 0 else acc[c] + part
+    owner_rows(micro - 1)
     for c in range(chunks):
         owner_sum(c)
         if c >= 1:
             x_sum(c - 1)
     x_sum(chunks - 1)
-    for c in range(chunks):
-        z_sum(c)
+    squares = z_sum(0)
+    for c in range(1, chunks):
+        squares += z_sum(c)
+    out[...] = out[...] * (clip_norm / jnp.maximum(jnp.sqrt(squares), clip_norm))
     labels_in.wait_send()
     for c in range(chunks):
         for s in range(micro):
@@ -318,13 +355,19 @@
     x_rows = nz * rows_dev
     chunks = width // CW
     vmem = pl.BlockSpec(memory_space=pltpu.VMEM)
+    hbm = pl.BlockSpec(memory_space=pl.ANY)
     dma = pltpu.SemaphoreType.DMA
-    row_grad = pl.pallas_call(
+    clipped = pl.pallas_call(
         functools.partial(kernel, dims),
         out_shape=jax.ShapeDtypeStruct((rows_dev, width), F32),
-        in_specs=[vmem, vmem, pl.BlockSpec(memory_space=pltpu.SMEM), vmem, vmem, vmem],
+        in_specs=[hbm, hbm, pl.BlockSpec(memory_space=pltpu.SMEM), hbm, hbm, hbm],
         out_specs=vmem,
         scratch_shapes=[
+            pltpu.VMEM(tokens.shape, BF),
+            pltpu.VMEM(cotangent.shape, BF),
+            pltpu.VMEM(item_rows.shape, I32),
+            pltpu.VMEM(w_in.shape, BF),
+            pltpu.VMEM(w_out.shape, BF),
             pltpu.VMEM((positions, 4 * width), BF),
             pltpu.VMEM((positions, 4 * width), F32),
             pltpu.VMEM((HEADS, positions, positions), BF),
@@ -346,6 +389,7 @@
             pltpu.VMEM((chunks, x_rows, CW), F32),
             pltpu.VMEM((chunks, x_rows, CW), BF),
             pltpu.VMEM((chunks, nz - 1, rows_dev, CW), BF),
+            dma((6 + 2 * micro,)),
             dma((2,)),
             dma((micro, chunks)),
             dma((micro, chunks)),
@@ -357,7 +401,7 @@
         compiler_params=pltpu.CompilerParams(collective_id=0, has_side_effects=True, vmem_limit_bytes=56 * 1024 * 1024),
         name="layer_rows",
     )(tokens, cotangent, lengths, item_rows, w_in, w_out)
-    return adam_rows(row_grad, table, moment_one, moment_two)
+    return adam_rows(clipped, table, moment_one, moment_two)
 
 
 def solution(mesh, x_chips=X_CHIPS, cores=2, rows_dev=32):

time: 60.8 us -> 59.4 us (0.977)
  other arithmetic: 2.58 us -> 1.53 us
    reduce_sum x1 -> x0, other arithmetic: 0.95 us -> none  [adam_rows(): row_norms = jnp.sqrt(jnp.sum(row_grad * row_grad, axis=1, keepdims=True))]
where the time goes in v2:
time: 59.4 us; the launch traced here: 59.2 us
  Pallas kernels  56.9 us (96%)
  other arithmetic  1.53 us (3%)
  between operations  0.69 us (1%)
    pallas_call x1, Pallas kernels, on_device(): pl.pallas_call(functools.partial(kernel, dims), out_shape=jax.ShapeDtypeS...  56.9 us
    sub x1, other arithmetic, adam_rows(): table - step_size * first_moment / scaled  1.53 us

profile of v2, /device:TPU:1, one launch (start us, length us, event | category | flops | bytes accessed | tf_op | source)
XLA Modules:
  0.0 59.2 jit_solution(11426781001088608797)
XLA Ops:
  0.6 0.0 copy-start.2
  0.6 0.0 copy-start.1
  0.7 0.0 copy-start
  0.7 56.9 %layer_rows.1 = f32[32,512]{1,0:T(8,128)} custom-call(bf16[2,256,512]{2,1,0:T(8,128)(2,1)} %tokens_hbm.1, bf16[2,256,512]{2,1,0:T(8,128)(2,1)} %cot_hbm.1, s32[2]{0:T(128)} %lengths.1, s32[2,256]{1,0:T(2,128)} %items_hbm.1, bf16[512,2048]{1,0:T(8,128)(2,1)} %w_in_hbm.1, bf16[512,512]{1,0:T(8,128)(2,1)} %w_out_hbm.1), custom_call_target="tpu_custom_call" | custom-call | tf_op jit(solution)/shard_map/layer_rows/pallas_call | solution.py:360
  57.6 0.0 copy-done.2
  57.6 0.0 copy-done.1
  57.6 0.0 copy-done
  57.6 1.5 %divide_subtract_fusion = (f32[32,512]{1,0:T(8,128)}, f32[32,512]{1,0:T(8,128)}, f32[32,512]{1,0:T(8,128)}) fusion(f32[32,512]{1,0:T(8,128)S(1)} %copy-done, f32[32,512]{1,0:T(8,128)} %layer_rows.1, f32[32,512]{1,0:T(8,128)S(1)} %copy-done.1, f32[32,512]{1,0:T(8,128)S(1)} %copy-done.2), kind=kLoop, calls=%fused_computation.2 | loop fusion | flops 196608 | bytes 458752 | tf_op jit(solution)/shard_map/sub | solution.py:44
Async XLA Ops:
  0.6 57.0 %copy-start.2 = (f32[32,512]{1,0:T(8,128)S(1)}, f32[32,512]{1,0:T(8,128)}, u32[]{:S(2)}) copy-start(f32[32,512]{1,0:T(8,128)} %param.17) | copy-start | bytes 196612
  0.6 57.0 %copy-start.1 = (f32[32,512]{1,0:T(8,128)S(1)}, f32[32,512]{1,0:T(8,128)}, u32[]{:S(2)}) copy-start(f32[32,512]{1,0:T(8,128)} %param.16) | copy-start | bytes 196612
  0.7 57.0 %copy-start = (f32[32,512]{1,0:T(8,128)S(1)}, f32[32,512]{1,0:T(8,128)}, u32[]{:S(2)}) copy-start(f32[32,512]{1,0:T(8,128)} %param.15) | copy-start | bytes 196612

commit v3 on v2

--- a/solution.py
+++ b/solution.py
@@ -163,9 +163,9 @@
 def kernel(
     dims, tokens_hbm, cot_hbm, lengths, items_hbm, w_in_hbm, w_out_hbm, out,
     tokens, cot, items, w_in, w_out,
-    hid, der, att, fac, mixed, ds, dmx, dinner, wmask, pack, lab_send, lab_recv, onehot,
-    send_y, recv_y, acc, send_x, recv_x, own_z, send_z, recv_z,
-    sem_in, sem_lab, sem_y_send, sem_y_recv, sem_x_send, sem_x_recv, sem_z_send, sem_z_recv,
+    hid, der, att, fac, mixed, ds, dmx, dinner, wmask, pack, lab_send, lab_recv, lab_near, onehot, onehot_near, recv_near,
+    send_y, recv_y, acc, send_x, recv_x, own_z, send_z, recv_z, send_far, recv_far,
+    sem_in, sem_lab, sem_near, sem_far, sem_y_send, sem_y_recv, sem_x_send, sem_x_recv, sem_z_send, sem_z_recv,
 ):
     nx, nz, ny, cores, rows_dev = dims
     micro, positions, width = tokens.shape
@@ -206,6 +206,15 @@
     hops = sorted(((dy, dc) for dy in range(ny) for dc in range(cores)), key=lambda h: (-min(h[0], ny - h[0]), h[1], h[0]))
     hops.remove((0, 0))
     near = [((my_y + dy) & (ny - 1)) * cores + ((my_core + dc) & (cores - 1)) for dy, dc in hops]
+    quarter = ny // 4
+    ahead = [0] + [sign * d for d in range(1, quarter) for sign in (1, -1)]
+    if quarter:
+        ahead.append(quarter - 2 * quarter * my_core)
+    close = [((my_y + dy) & (ny - 1)) * cores + ((my_core + dc) & (cores - 1)) for dy in ahead for dc in range(cores)]
+
+    def opposite(owner):
+        return (owner + owners // 2) & (owners - 1)
+
     x_peers = [(my_x + d) & (nx - 1) for d in range(1, nx)]
     z_peers = [(my_z + d) & (nz - 1) for d in range(1, nz)]
 
@@ -223,11 +232,36 @@
     for h in range(2):
         ds[h, :half, half:] = jnp.zeros((half, half), BF)
 
-    lab_send[...] = jnp.zeros(lab_send.shape, F32)
     copies["items",].wait()
     for s in range(micro):
         layout_rows(s, items, owners, cap, rows_dev, pack, lab_send)
     lab_recv[0] = lab_send[narrow]
+    lab_near[0, 0] = lab_send[narrow]
+    lab_near[1, 0] = lab_send[opposite(narrow)]
+
+    def slots_of(owner):
+        return pl.ds(pl.multiple_of(owner * cap, cap), cap)
+
+    def send_rows(s, c):
+        for k, peer in enumerate(near):
+            pltpu.make_async_remote_copy(
+                send_y.at[s, c, slots_of(peer)], recv_y.at[s, c, pl.ds((k + 1) * cap, cap)],
+                sem_y_send.at[s, c], sem_y_recv.at[s, c],
+                device_id=(wide, peer), device_id_type=MESH,
+            ).start()
+        recv_y[s, c, :cap] = send_y[s, c, slots_of(narrow), :]
+
+    def send_rows_near(s):
+        for k, peer in enumerate(close):
+            for g, owner in enumerate((peer, opposite(peer))):
+                if k == 0:
+                    recv_near[s, g, :cap] = send_y[s, 0, slots_of(owner), :]
+                else:
+                    pltpu.make_async_remote_copy(
+                        send_y.at[s, 0, slots_of(owner)], recv_near.at[s, g, pl.ds(k * cap, cap)],
+                        sem_near.at[0, s, g], sem_near.at[1, s, g],
+                        device_id=(wide, peer), device_id_type=MESH,
+                    ).start()
 
     def one_sequence(s, carry):
         live = sequence_grad(s, tokens, cot, lengths, w_in, w_out, arrived, hid, der, att, fac, mixed, ds, dmx, dinner, wmask)
@@ -240,6 +274,12 @@
                     lab_send.at[peer], lab_recv.at[k + 1], sem_lab.at[0], sem_lab.at[1],
                     device_id=(wide, peer), device_id_type=MESH,
                 ).start()
+            for k, peer in enumerate(close[1:], 1):
+                for g, owner in enumerate((peer, opposite(peer))):
+                    pltpu.make_async_remote_copy(
+                        lab_send.at[owner], lab_near.at[g, k], sem_lab.at[2], sem_lab.at[3],
+                        device_id=(wide, peer), device_id_type=MESH,
+                    ).start()
 
         for w in range(width // 256):
             cols = slice(w * 256, (w + 1) * 256)
@@ -248,14 +288,14 @@
             packed = nn(pack[s], grad).astype(BF)
             for c in range(w * 256 // CW, (w + 1) * 256 // CW):
                 send_y[s, c] = packed[:, c * CW - w * 256 : (c + 1) * CW - w * 256]
-                for k, peer in enumerate(near):
-                    pltpu.make_async_remote_copy(
-                        send_y.at[s, c, pl.ds(pl.multiple_of(peer * cap, cap), cap)],
-                        recv_y.at[s, c, pl.ds((k + 1) * cap, cap)],
-                        sem_y_send.at[s, c], sem_y_recv.at[s, c],
-                        device_id=(wide, peer), device_id_type=MESH,
-                    ).start()
-                recv_y[s, c, :cap] = send_y[s, c, pl.ds(pl.multiple_of(narrow * cap, cap), cap), :]
+                if c == 0:
+                    send_rows_near(s)
+                    for earlier in range(micro - 1):
+                        pl.when(s == earlier + 1)(functools.partial(send_rows, earlier, chunks - 1))
+                elif c < chunks - 1:
+                    send_rows(s, c)
+                else:
+                    pl.when(s == micro - 1)(functools.partial(send_rows, micro - 1, c))
         return carry
 
     lax.fori_loop(0, micro, one_sequence, 0)
@@ -264,16 +304,25 @@
         return pltpu.make_async_remote_copy(src, dst, send, recv, device_id=(wide, narrow), device_id_type=MESH)
 
     labels_in = whole(lab_send.at[pl.ds(1, owners - 1)], lab_recv.at[pl.ds(1, owners - 1)], sem_lab.at[0], sem_lab.at[1])
+    near_count = 2 * (owners // 2 - 1)
+    labels_near = whole(lab_send.at[pl.ds(1, near_count)], lab_recv.at[pl.ds(1, near_count)], sem_lab.at[2], sem_lab.at[3])
+    labels_near.wait_recv()
     labels_in.wait_recv()
     group = 128 // cap
     lane = iota((1, 128), 1)
 
-    def owner_rows(s):
-        for g in range(slots // 128):
-            row = lab_recv[g * group, s : s + 1, :]
+    def owner_rows(s, count, labels):
+        blocks = []
+        for g in range(count // 128):
+            row = labels[g * group, s : s + 1, :]
             for k in range(1, group):
-                row = jnp.where(lane >= k * cap, lab_recv[g * group + k, s : s + 1, :], row)
-            onehot[s, :, g * 128 : (g + 1) * 128] = as_one(iota((owned, 128), 0) == row.astype(I32))
+                row = jnp.where(lane >= k * cap, labels[g * group + k, s : s + 1, :], row)
+            blocks.append(as_one(iota((owned, 128), 0) == row.astype(I32)))
+        return blocks
+
+    def near_copy(s, g):
+        rest = pl.ds(cap, slots // 2 - cap)
+        return whole(send_y.at[s, 0, rest], recv_near.at[s, g, rest], sem_near.at[0, s, g], sem_near.at[1, s, g])
 
     def y_copy(s, c):
         return whole(send_y.at[s, c, pl.ds(cap, slots - cap)], recv_y.at[s, c, pl.ds(cap, slots - cap)], sem_y_send.at[s, c], sem_y_recv.at[s, c])
@@ -294,12 +343,15 @@
             device_id=(my_x * nz + peer, narrow), device_id_type=MESH,
         )
 
+    def x_send(c):
+        send_x[c] = acc[c].astype(BF)
+        for d in range(nx - 1):
+            x_copy(c, d).start()
+
     def owner_sum(c):
         y_copy(micro - 1, c).wait_recv()
         acc[c] += nn(onehot[micro - 1], recv_y[micro - 1, c])
-        send_x[c] = acc[c].astype(BF)
-        for d in range(nx - 1):
-            x_copy(c, d).start()
+        x_send(c)
 
     def x_sum(c):
         total = acc[c, pl.ds(pl.multiple_of(my_x * x_rows, x_rows), x_rows), :]
@@ -316,29 +368,64 @@
         for d in range(nz - 1):
             z_copy(c, d).wait_recv()
             total += recv_z[c, d].astype(F32)
+        return total
+
+    def far_copy():
+        return pltpu.make_async_remote_copy(
+            send_far, recv_far, sem_far.at[0], sem_far.at[1],
+            device_id=(wide, opposite(narrow)), device_id_type=MESH,
+        )
+
+    def finish(c, total):
         out[:, c * CW : (c + 1) * CW] = total
         return jnp.sum(total * total, axis=1, keepdims=True)
 
+    for s in range(micro):
+        for g in range(2):
+            for i, block in enumerate(owner_rows(s, slots // 2, lab_near.at[g])):
+                onehot_near[s, g, :, i * 128 : (i + 1) * 128] = block
+    far = chunks
+    for s in range(micro):
+        for g, c in enumerate((0, far)):
+            near_copy(s, g).wait_recv()
+            part = nn(onehot_near[s, g], recv_near[s, g])
+            acc[c] = part if s == 0 else acc[c] + part
+            if s == micro - 1:
+                x_send(c)
+    for s in range(micro):
+        for i, block in enumerate(owner_rows(s, slots, lab_recv)):
+            onehot[s, :, i * 128 : (i + 1) * 128] = block
     for s in range(micro - 1):
-        owner_rows(s)
-        for c in range(chunks):
+        for c in range(1, chunks):
             y_copy(s, c).wait_recv()
             part = nn(onehot[s], recv_y[s, c])
             acc[c] = part if s == 0 else acc[c] + part
-    owner_rows(micro - 1)
-    for c in range(chunks):
+    x_sum(0)
+    owner_sum(1)
+    x_sum(far)
+    for c in range(2, chunks):
         owner_sum(c)
-        if c >= 1:
-            x_sum(c - 1)
+        x_sum(c - 1)
+    send_far[...] = z_sum(far).astype(BF)
+    far_copy().start()
     x_sum(chunks - 1)
-    squares = z_sum(0)
-    for c in range(1, chunks):
-        squares += z_sum(c)
+    squares = 0.0
+    for c in range(1, chunks - 1):
+        squares += finish(c, z_sum(c))
+    total = z_sum(0)
+    far_copy().wait_recv()
+    squares += finish(0, total + recv_far[...].astype(F32))
+    squares += finish(chunks - 1, z_sum(chunks - 1))
     out[...] = out[...] * (clip_norm / jnp.maximum(jnp.sqrt(squares), clip_norm))
     labels_in.wait_send()
-    for c in range(chunks):
-        for s in range(micro):
+    labels_near.wait_send()
+    far_copy().wait_send()
+    for s in range(micro):
+        for g in range(2):
+            near_copy(s, g).wait_send()
+        for c in range(1, chunks):
             y_copy(s, c).wait_send()
+    for c in range(chunks + 1):
         for d in range(nx - 1):
             x_copy(c, d).wait_send()
         for d in range(nz - 1):
@@ -378,25 +465,32 @@
             pltpu.VMEM((positions, 4 * width), BF),
             pltpu.VMEM((3, positions // 2, positions // 2), F32),
             pltpu.VMEM((micro, slots, positions), BF),
-            pltpu.VMEM((owners, 8, 128), F32),
-            pltpu.VMEM((owners, 8, 128), F32),
+            pltpu.VMEM((owners, micro, 128), F32),
+            pltpu.VMEM((owners, micro, 128), F32),
+            pltpu.VMEM((2, owners // 2, micro, 128), F32),
             pltpu.VMEM((micro, owned, slots), BF),
+            pltpu.VMEM((micro, 2, owned, slots // 2), BF),
+            pltpu.VMEM((micro, 2, slots // 2, CW), BF),
             pltpu.VMEM((micro, chunks, slots, CW), BF),
             pltpu.VMEM((micro, chunks, slots, CW), BF),
-            pltpu.VMEM((chunks, owned, CW), F32),
-            pltpu.VMEM((chunks, owned, CW), BF),
-            pltpu.VMEM((chunks, nx - 1, x_rows, CW), BF),
-            pltpu.VMEM((chunks, x_rows, CW), F32),
-            pltpu.VMEM((chunks, x_rows, CW), BF),
-            pltpu.VMEM((chunks, nz - 1, rows_dev, CW), BF),
+            pltpu.VMEM((chunks + 1, owned, CW), F32),
+            pltpu.VMEM((chunks + 1, owned, CW), BF),
+            pltpu.VMEM((chunks + 1, max(nx - 1, 1), x_rows, CW), BF),
+            pltpu.VMEM((chunks + 1, x_rows, CW), F32),
+            pltpu.VMEM((chunks + 1, x_rows, CW), BF),
+            pltpu.VMEM((chunks + 1, max(nz - 1, 1), rows_dev, CW), BF),
+            pltpu.VMEM((rows_dev, CW), BF),
+            pltpu.VMEM((rows_dev, CW), BF),
             dma((6 + 2 * micro,)),
+            dma((4,)),
+            dma((2, micro, 2)),
             dma((2,)),
             dma((micro, chunks)),
             dma((micro, chunks)),
-            dma((chunks, nx - 1)),
-            dma((chunks, nx - 1)),
-            dma((chunks, nz - 1)),
-            dma((chunks, nz - 1)),
+            dma((chunks + 1, max(nx - 1, 1))),
+            dma((chunks + 1, max(nx - 1, 1))),
+            dma((chunks + 1, max(nz - 1, 1))),
+            dma((chunks + 1, max(nz - 1, 1))),
         ],
         compiler_params=pltpu.CompilerParams(collective_id=0, has_side_effects=True, vmem_limit_bytes=56 * 1024 * 1024),
         name="layer_rows",

time: 59.4 us -> 58.3 us (0.981)
  Pallas kernels: 56.9 us -> 55.6 us
    pallas_call x1, Pallas kernels: 56.9 us -> 55.6 us  [on_device(): pl.pallas_call(functools.partial(kernel, dims), out_shape=jax.ShapeDtypeS...]
where the time goes in v3:
time: 58.3 us; the launch traced here: 57.9 us
  Pallas kernels  55.6 us (95%)
  other arithmetic  1.53 us (3%)
  between operations  0.69 us (1%)
    pallas_call x1, Pallas kernels, on_device(): pl.pallas_call(functools.partial(kernel, dims), out_shape=jax.ShapeDtypeS...  55.6 us
    sub x1, other arithmetic, adam_rows(): table - step_size * first_moment / scaled  1.53 us

profile of v3, /device:TPU:1, one launch (start us, length us, event | category | flops | bytes accessed | tf_op | source)
XLA Modules:
  0.0 57.9 jit_solution(1380573287300966462)
XLA Ops:
  0.6 0.0 copy-start.2
  0.6 0.0 copy-start.1
  0.7 0.0 copy-start
  0.7 55.6 %layer_rows.1 = f32[32,512]{1,0:T(8,128)} custom-call(bf16[2,256,512]{2,1,0:T(8,128)(2,1)} %tokens_hbm.1, bf16[2,256,512]{2,1,0:T(8,128)(2,1)} %cot_hbm.1, s32[2]{0:T(128)} %lengths.1, s32[2,256]{1,0:T(2,128)} %items_hbm.1, bf16[512,2048]{1,0:T(8,128)(2,1)} %w_in_hbm.1, bf16[512,512]{1,0:T(8,128)(2,1)} %w_out_hbm.1), custom_call_target="tpu_custom_call" | custom-call | tf_op jit(solution)/shard_map/layer_rows/pallas_call | solution.py:447
  56.3 0.0 copy-done.2
  56.3 0.0 copy-done.1
  56.3 0.0 copy-done
  56.3 1.5 %divide_subtract_fusion = (f32[32,512]{1,0:T(8,128)}, f32[32,512]{1,0:T(8,128)}, f32[32,512]{1,0:T(8,128)}) fusion(f32[32,512]{1,0:T(8,128)S(1)} %copy-done, f32[32,512]{1,0:T(8,128)} %layer_rows.1, f32[32,512]{1,0:T(8,128)S(1)} %copy-done.1, f32[32,512]{1,0:T(8,128)S(1)} %copy-done.2), kind=kLoop, calls=%fused_computation.2 | loop fusion | flops 196608 | bytes 458752 | tf_op jit(solution)/shard_map/sub | solution.py:44
Async XLA Ops:
  0.6 55.7 %copy-start.2 = (f32[32,512]{1,0:T(8,128)S(1)}, f32[32,512]{1,0:T(8,128)}, u32[]{:S(2)}) copy-start(f32[32,512]{1,0:T(8,128)} %param.17) | copy-start | bytes 196612
  0.6 55.7 %copy-start.1 = (f32[32,512]{1,0:T(8,128)S(1)}, f32[32,512]{1,0:T(8,128)}, u32[]{:S(2)}) copy-start(f32[32,512]{1,0:T(8,128)} %param.16) | copy-start | bytes 196612
  0.7 55.7 %copy-start = (f32[32,512]{1,0:T(8,128)S(1)}, f32[32,512]{1,0:T(8,128)}, u32[]{:S(2)}) copy-start(f32[32,512]{1,0:T(8,128)} %param.15) | copy-start | bytes 196612

commit v4 on v3

--- a/solution.py
+++ b/solution.py
@@ -13,6 +13,7 @@
 I32 = jnp.int32
 MESH = pl.DeviceIdType.MESH
 CW = 128
+SHORT = 2
 X_CHIPS = 4
 
 norm_eps = 1e-06
@@ -164,8 +165,8 @@
     dims, tokens_hbm, cot_hbm, lengths, items_hbm, w_in_hbm, w_out_hbm, out,
     tokens, cot, items, w_in, w_out,
     hid, der, att, fac, mixed, ds, dmx, dinner, wmask, pack, lab_send, lab_recv, lab_near, onehot, onehot_near, recv_near,
-    send_y, recv_y, acc, send_x, recv_x, own_z, send_z, recv_z, send_far, recv_far,
-    sem_in, sem_lab, sem_near, sem_far, sem_y_send, sem_y_recv, sem_x_send, sem_x_recv, sem_z_send, sem_z_recv,
+    send_y, recv_y, acc, send_x, recv_x, own_z, send_z, recv_z, send_zf, recv_zf, own_xf, send_xf, recv_xf, send_far, recv_far,
+    sem_in, sem_lab, sem_near, sem_far, sem_zf, sem_xf, sem_sub, sem_y_send, sem_y_recv, sem_x_send, sem_x_recv, sem_z_send, sem_z_recv,
 ):
     nx, nz, ny, cores, rows_dev = dims
     micro, positions, width = tokens.shape
@@ -251,15 +252,15 @@
             ).start()
         recv_y[s, c, :cap] = send_y[s, c, slots_of(narrow), :]
 
-    def send_rows_near(s):
+    def send_rows_near(s, c):
         for k, peer in enumerate(close):
             for g, owner in enumerate((peer, opposite(peer))):
                 if k == 0:
-                    recv_near[s, g, :cap] = send_y[s, 0, slots_of(owner), :]
+                    recv_near[s, c, g, :cap] = send_y[s, c, slots_of(owner), :]
                 else:
                     pltpu.make_async_remote_copy(
-                        send_y.at[s, 0, slots_of(owner)], recv_near.at[s, g, pl.ds(k * cap, cap)],
-                        sem_near.at[0, s, g], sem_near.at[1, s, g],
+                        send_y.at[s, c, slots_of(owner)], recv_near.at[s, c, g, pl.ds(k * cap, cap)],
+                        sem_near.at[0, s, c, g], sem_near.at[1, s, c, g],
                         device_id=(wide, peer), device_id_type=MESH,
                     ).start()
 
@@ -288,13 +289,14 @@
             packed = nn(pack[s], grad).astype(BF)
             for c in range(w * 256 // CW, (w + 1) * 256 // CW):
                 send_y[s, c] = packed[:, c * CW - w * 256 : (c + 1) * CW - w * 256]
-                if c == 0:
-                    send_rows_near(s)
+                if c < SHORT:
+                    send_rows_near(s, c)
+                if c == SHORT - 1:
                     for earlier in range(micro - 1):
                         pl.when(s == earlier + 1)(functools.partial(send_rows, earlier, chunks - 1))
-                elif c < chunks - 1:
+                if SHORT <= c < chunks - 1:
                     send_rows(s, c)
-                else:
+                if c == chunks - 1:
                     pl.when(s == micro - 1)(functools.partial(send_rows, micro - 1, c))
         return carry
 
@@ -320,9 +322,9 @@
             blocks.append(as_one(iota((owned, 128), 0) == row.astype(I32)))
         return blocks
 
-    def near_copy(s, g):
+    def near_copy(s, c, g):
         rest = pl.ds(cap, slots // 2 - cap)
-        return whole(send_y.at[s, 0, rest], recv_near.at[s, g, rest], sem_near.at[0, s, g], sem_near.at[1, s, g])
+        return whole(send_y.at[s, c, rest], recv_near.at[s, c, g, rest], sem_near.at[0, s, c, g], sem_near.at[1, s, c, g])
 
     def y_copy(s, c):
         return whole(send_y.at[s, c, pl.ds(cap, slots - cap)], recv_y.at[s, c, pl.ds(cap, slots - cap)], sem_y_send.at[s, c], sem_y_recv.at[s, c])
@@ -343,10 +345,78 @@
             device_id=(my_x * nz + peer, narrow), device_id_type=MESH,
         )
 
+    last = chunks - 1
+    parts = min(nz, 4)
+    part_rows = x_rows // parts
+
+    def sub_copy(q, d):
+        peer = x_peers[d]
+        rows = pl.ds(pl.multiple_of(peer * x_rows + q * part_rows, part_rows), part_rows)
+        return pltpu.make_async_remote_copy(
+            send_x.at[last, rows], recv_x.at[last, d, pl.ds(q * part_rows, part_rows)],
+            sem_sub.at[0, q, d], sem_sub.at[1, q, d],
+            device_id=(peer * nz + my_z, narrow), device_id_type=MESH,
+        )
+
+    def zf_copy(d):
+        peer = z_peers[d]
+        return pltpu.make_async_remote_copy(
+            send_zf.at[:, peer], recv_zf.at[d], sem_zf.at[0, d], sem_zf.at[1, d],
+            device_id=(my_x * nz + peer, narrow), device_id_type=MESH,
+        )
+
+    def xf_copy(d):
+        peer = x_peers[d]
+        return pltpu.make_async_remote_copy(
+            send_xf.at[peer], recv_xf.at[d], sem_xf.at[0, d], sem_xf.at[1, d],
+            device_id=(peer * nz + my_z, narrow), device_id_type=MESH,
+        )
+
+    def zf_send(c):
+        send_zf[...] = acc[c].astype(BF).reshape(send_zf.shape)
+        for d in range(nz - 1):
+            zf_copy(d).start()
+
+    def zf_sum(c):
+        rows = [acc[c, pl.ds(pl.multiple_of(x * x_rows + my_z * rows_dev, rows_dev), rows_dev), :] for x in range(nx)]
+        for d in range(nz - 1):
+            zf_copy(d).wait_recv()
+        for x in range(nx):
+            total = rows[x]
+            for d in range(nz - 1):
+                total += recv_zf[d, x].astype(F32)
+            own_xf[x] = total
+            send_xf[x] = total.astype(BF)
+        for d in range(nx - 1):
+            xf_copy(d).start()
+
+    def xf_sum():
+        total = own_xf[my_x]
+        for d in range(nx - 1):
+            xf_copy(d).wait_recv()
+            total += recv_xf[d].astype(F32)
+        return total
+
     def x_send(c):
         send_x[c] = acc[c].astype(BF)
+        if c == last:
+            for q in range(parts):
+                for d in range(nx - 1):
+                    sub_copy(q, d).start()
+        else:
+            for d in range(nx - 1):
+                x_copy(c, d).start()
+
+    def sub_sum(q):
+        rows = slice(q * part_rows, (q + 1) * part_rows)
+        total = acc[last, pl.ds(pl.multiple_of(my_x * x_rows + q * part_rows, part_rows), part_rows), :]
         for d in range(nx - 1):
-            x_copy(c, d).start()
+            sub_copy(q, d).wait_recv()
+            total += recv_x[last, d, rows].astype(F32)
+        own_z[last, rows] = total
+        send_z[last, rows] = total.astype(BF)
+        for d in range(nz - 1):
+            pl.when((z_peers[d] >> bits(nz // parts)) == q)(z_copy(last, d).start)
 
     def owner_sum(c):
         y_copy(micro - 1, c).wait_recv()
@@ -370,9 +440,9 @@
             total += recv_z[c, d].astype(F32)
         return total
 
-    def far_copy():
+    def far_copy(i):
         return pltpu.make_async_remote_copy(
-            send_far, recv_far, sem_far.at[0], sem_far.at[1],
+            send_far.at[i], recv_far.at[i], sem_far.at[0, i], sem_far.at[1, i],
             device_id=(wide, opposite(narrow)), device_id_type=MESH,
         )
 
@@ -384,50 +454,65 @@
         for g in range(2):
             for i, block in enumerate(owner_rows(s, slots // 2, lab_near.at[g])):
                 onehot_near[s, g, :, i * 128 : (i + 1) * 128] = block
-    far = chunks
-    for s in range(micro):
-        for g, c in enumerate((0, far)):
-            near_copy(s, g).wait_recv()
-            part = nn(onehot_near[s, g], recv_near[s, g])
-            acc[c] = part if s == 0 else acc[c] + part
-            if s == micro - 1:
-                x_send(c)
+    for c in range(SHORT):
+        for s in range(micro):
+            for g, table in enumerate((c, chunks + c)):
+                near_copy(s, c, g).wait_recv()
+                part = nn(onehot_near[s, g], recv_near[s, c, g])
+                acc[table] = part if s == 0 else acc[table] + part
+        if c == 0:
+            zf_send(chunks)
+        else:
+            x_send(chunks + c)
+        x_send(c)
     for s in range(micro):
         for i, block in enumerate(owner_rows(s, slots, lab_recv)):
             onehot[s, :, i * 128 : (i + 1) * 128] = block
     for s in range(micro - 1):
-        for c in range(1, chunks):
+        for c in range(SHORT, chunks):
             y_copy(s, c).wait_recv()
             part = nn(onehot[s], recv_y[s, c])
             acc[c] = part if s == 0 else acc[c] + part
     x_sum(0)
-    owner_sum(1)
-    x_sum(far)
-    for c in range(2, chunks):
-        owner_sum(c)
-        x_sum(c - 1)
-    send_far[...] = z_sum(far).astype(BF)
-    far_copy().start()
-    x_sum(chunks - 1)
-    squares = 0.0
-    for c in range(1, chunks - 1):
-        squares += finish(c, z_sum(c))
-    total = z_sum(0)
-    far_copy().wait_recv()
-    squares += finish(0, total + recv_far[...].astype(F32))
-    squares += finish(chunks - 1, z_sum(chunks - 1))
+    owner_sum(2)
+    x_sum(chunks + 1)
+    x_sum(1)
+    zf_sum(chunks)
+    owner_sum(3)
+    send_far[0] = xf_sum().astype(BF)
+    far_copy(0).start()
+    x_sum(2)
+    send_far[1] = z_sum(chunks + 1).astype(BF)
+    far_copy(1).start()
+    for q in range(parts):
+        sub_sum(q)
+    squares = finish(2, z_sum(2))
+    for c in range(SHORT):
+        total = z_sum(c)
+        far_copy(c).wait_recv()
+        squares += finish(c, total + recv_far[c].astype(F32))
+    squares += finish(last, z_sum(last))
     out[...] = out[...] * (clip_norm / jnp.maximum(jnp.sqrt(squares), clip_norm))
     labels_in.wait_send()
     labels_near.wait_send()
-    far_copy().wait_send()
     for s in range(micro):
-        for g in range(2):
-            near_copy(s, g).wait_send()
-        for c in range(1, chunks):
+        for c in range(SHORT):
+            for g in range(2):
+                near_copy(s, c, g).wait_send()
+        for c in range(SHORT, chunks):
             y_copy(s, c).wait_send()
-    for c in range(chunks + 1):
-        for d in range(nx - 1):
-            x_copy(c, d).wait_send()
+    for c in range(SHORT):
+        far_copy(c).wait_send()
+    for d in range(nz - 1):
+        zf_copy(d).wait_send()
+    for d in range(nx - 1):
+        xf_copy(d).wait_send()
+        for q in range(parts):
+            sub_copy(q, d).wait_send()
+    for c in (0, 1, 2, 3, chunks + 1):
+        if c != last:
+            for d in range(nx - 1):
+                x_copy(c, d).wait_send()
         for d in range(nz - 1):
             z_copy(c, d).wait_send()
 
@@ -470,27 +555,35 @@
             pltpu.VMEM((2, owners // 2, micro, 128), F32),
             pltpu.VMEM((micro, owned, slots), BF),
             pltpu.VMEM((micro, 2, owned, slots // 2), BF),
-            pltpu.VMEM((micro, 2, slots // 2, CW), BF),
+            pltpu.VMEM((micro, SHORT, 2, slots // 2, CW), BF),
             pltpu.VMEM((micro, chunks, slots, CW), BF),
             pltpu.VMEM((micro, chunks, slots, CW), BF),
-            pltpu.VMEM((chunks + 1, owned, CW), F32),
-            pltpu.VMEM((chunks + 1, owned, CW), BF),
-            pltpu.VMEM((chunks + 1, max(nx - 1, 1), x_rows, CW), BF),
-            pltpu.VMEM((chunks + 1, x_rows, CW), F32),
-            pltpu.VMEM((chunks + 1, x_rows, CW), BF),
-            pltpu.VMEM((chunks + 1, max(nz - 1, 1), rows_dev, CW), BF),
-            pltpu.VMEM((rows_dev, CW), BF),
-            pltpu.VMEM((rows_dev, CW), BF),
+            pltpu.VMEM((chunks + 2, owned, CW), F32),
+            pltpu.VMEM((chunks + 2, owned, CW), BF),
+            pltpu.VMEM((chunks + 2, max(nx - 1, 1), x_rows, CW), BF),
+            pltpu.VMEM((chunks + 2, x_rows, CW), F32),
+            pltpu.VMEM((chunks + 2, x_rows, CW), BF),
+            pltpu.VMEM((chunks + 2, max(nz - 1, 1), rows_dev, CW), BF),
+            pltpu.VMEM((nx, nz, rows_dev, CW), BF),
+            pltpu.VMEM((max(nz - 1, 1), nx, rows_dev, CW), BF),
+            pltpu.VMEM((nx, rows_dev, CW), F32),
+            pltpu.VMEM((nx, rows_dev, CW), BF),
+            pltpu.VMEM((max(nx - 1, 1), rows_dev, CW), BF),
+            pltpu.VMEM((2, rows_dev, CW), BF),
+            pltpu.VMEM((2, rows_dev, CW), BF),
             dma((6 + 2 * micro,)),
             dma((4,)),
-            dma((2, micro, 2)),
-            dma((2,)),
+            dma((2, micro, SHORT, 2)),
+            dma((2, 2)),
+            dma((2, max(nz - 1, 1))),
+            dma((2, max(nx - 1, 1))),
+            dma((2, min(nz, 4), max(nx - 1, 1))),
             dma((micro, chunks)),
             dma((micro, chunks)),
-            dma((chunks + 1, max(nx - 1, 1))),
-            dma((chunks + 1, max(nx - 1, 1))),
-            dma((chunks + 1, max(nz - 1, 1))),
-            dma((chunks + 1, max(nz - 1, 1))),
+            dma((chunks + 2, max(nx - 1, 1))),
+            dma((chunks + 2, max(nx - 1, 1))),
+            dma((chunks + 2, max(nz - 1, 1))),
+            dma((chunks + 2, max(nz - 1, 1))),
         ],
         compiler_params=pltpu.CompilerParams(collective_id=0, has_side_effects=True, vmem_limit_bytes=56 * 1024 * 1024),
         name="layer_rows",

time: 58.3 us -> 58 us (level)
  no operation moved by 1% of the time
where the time goes in v4:
time: 58 us; the launch traced here: 57.8 us
  Pallas kernels  55.5 us (96%)
  other arithmetic  1.53 us (3%)
  between operations  0.69 us (1%)
    pallas_call x1, Pallas kernels, on_device(): pl.pallas_call(functools.partial(kernel, dims), out_shape=jax.ShapeDtypeS...  55.5 us
    sub x1, other arithmetic, adam_rows(): table - step_size * first_moment / scaled  1.53 us

profile of v4, /device:TPU:1, one launch (start us, length us, event | category | flops | bytes accessed | tf_op | source)
XLA Modules:
  0.0 57.8 jit_solution(16063014281635074031)
XLA Ops:
  0.6 0.0 copy-start.2
  0.6 0.0 copy-start.1
  0.7 0.0 copy-start
  0.7 55.5 %layer_rows.1 = f32[32,512]{1,0:T(8,128)} custom-call(bf16[2,256,512]{2,1,0:T(8,128)(2,1)} %tokens_hbm.1, bf16[2,256,512]{2,1,0:T(8,128)(2,1)} %cot_hbm.1, s32[2]{0:T(128)} %lengths.1, s32[2,256]{1,0:T(2,128)} %items_hbm.1, bf16[512,2048]{1,0:T(8,128)(2,1)} %w_in_hbm.1, bf16[512,512]{1,0:T(8,128)(2,1)} %w_out_hbm.1), custom_call_target="tpu_custom_call" | custom-call | tf_op jit(solution)/shard_map/layer_rows/pallas_call | solution.py:532
  56.2 0.0 copy-done.2
  56.2 0.0 copy-done.1
  56.2 0.0 copy-done
  56.2 1.5 %divide_subtract_fusion = (f32[32,512]{1,0:T(8,128)}, f32[32,512]{1,0:T(8,128)}, f32[32,512]{1,0:T(8,128)}) fusion(f32[32,512]{1,0:T(8,128)S(1)} %copy-done, f32[32,512]{1,0:T(8,128)} %layer_rows.1, f32[32,512]{1,0:T(8,128)S(1)} %copy-done.1, f32[32,512]{1,0:T(8,128)S(1)} %copy-done.2), kind=kLoop, calls=%fused_computation.2 | loop fusion | flops 196608 | bytes 458752 | tf_op jit(solution)/shard_map/sub | solution.py:45
Async XLA Ops:
  0.6 55.6 %copy-start.2 = (f32[32,512]{1,0:T(8,128)S(1)}, f32[32,512]{1,0:T(8,128)}, u32[]{:S(2)}) copy-start(f32[32,512]{1,0:T(8,128)} %param.17) | copy-start | bytes 196612
  0.6 55.6 %copy-start.1 = (f32[32,512]{1,0:T(8,128)S(1)}, f32[32,512]{1,0:T(8,128)}, u32[]{:S(2)}) copy-start(f32[32,512]{1,0:T(8,128)} %param.16) | copy-start | bytes 196612
  0.7 55.6 %copy-start = (f32[32,512]{1,0:T(8,128)S(1)}, f32[32,512]{1,0:T(8,128)}, u32[]{:S(2)}) copy-start(f32[32,512]{1,0:T(8,128)} %param.15) | copy-start | bytes 196612

commit v5 on v4

--- a/solution.py
+++ b/solution.py
@@ -291,16 +291,12 @@
                 send_y[s, c] = packed[:, c * CW - w * 256 : (c + 1) * CW - w * 256]
                 if c < SHORT:
                     send_rows_near(s, c)
-                if c == SHORT - 1:
-                    for earlier in range(micro - 1):
-                        pl.when(s == earlier + 1)(functools.partial(send_rows, earlier, chunks - 1))
-                if SHORT <= c < chunks - 1:
-                    send_rows(s, c)
-                if c == chunks - 1:
-                    pl.when(s == micro - 1)(functools.partial(send_rows, micro - 1, c))
+                if c == SHORT:
+                    pl.when(s < micro - 1)(functools.partial(send_rows, s, c))
         return carry
 
     lax.fori_loop(0, micro, one_sequence, 0)
+    send_rows(0, chunks - 1)
 
     def whole(src, dst, send, recv):
         return pltpu.make_async_remote_copy(src, dst, send, recv, device_id=(wide, narrow), device_id_type=MESH)
@@ -461,10 +457,12 @@
                 part = nn(onehot_near[s, g], recv_near[s, c, g])
                 acc[table] = part if s == 0 else acc[table] + part
         if c == 0:
+            send_rows(1, SHORT)
             zf_send(chunks)
         else:
             x_send(chunks + c)
         x_send(c)
+    send_rows(1, chunks - 1)
     for s in range(micro):
         for i, block in enumerate(owner_rows(s, slots, lab_recv)):
             onehot[s, :, i * 128 : (i + 1) * 128] = block

time: 58 us -> 56.8 us (0.979)
  Pallas kernels: 55.5 us -> 54.2 us
    pallas_call x1, Pallas kernels: 55.5 us -> 54.2 us  [on_device(): pl.pallas_call(functools.partial(kernel, dims), out_shape=jax.ShapeDtypeS...]
where the time goes in v5:
time: 56.8 us; the launch traced here: 56.4 us
  Pallas kernels  54.2 us (95%)
  other arithmetic  1.53 us (3%)
  between operations  0.69 us (1%)
    pallas_call x1, Pallas kernels, on_device(): pl.pallas_call(functools.partial(kernel, dims), out_shape=jax.ShapeDtypeS...  54.2 us
    sub x1, other arithmetic, adam_rows(): table - step_size * first_moment / scaled  1.53 us

profile of v5, /device:TPU:1, one launch (start us, length us, event | category | flops | bytes accessed | tf_op | source)
XLA Modules:
  0.0 56.4 jit_solution(17311885393806030387)
XLA Ops:
  0.6 0.0 copy-start.2
  0.6 0.0 copy-start.1
  0.7 0.0 copy-start
  0.7 54.2 %layer_rows.1 = f32[32,512]{1,0:T(8,128)} custom-call(bf16[2,256,512]{2,1,0:T(8,128)(2,1)} %tokens_hbm.1, bf16[2,256,512]{2,1,0:T(8,128)(2,1)} %cot_hbm.1, s32[2]{0:T(128)} %lengths.1, s32[2,256]{1,0:T(2,128)} %items_hbm.1, bf16[512,2048]{1,0:T(8,128)(2,1)} %w_in_hbm.1, bf16[512,512]{1,0:T(8,128)(2,1)} %w_out_hbm.1), custom_call_target="tpu_custom_call" | custom-call | tf_op jit(solution)/shard_map/layer_rows/pallas_call | solution.py:530
  54.8 0.0 copy-done.2
  54.8 0.0 copy-done.1
  54.9 0.0 copy-done
  54.9 1.5 %divide_subtract_fusion = (f32[32,512]{1,0:T(8,128)}, f32[32,512]{1,0:T(8,128)}, f32[32,512]{1,0:T(8,128)}) fusion(f32[32,512]{1,0:T(8,128)S(1)} %copy-done, f32[32,512]{1,0:T(8,128)} %layer_rows.1, f32[32,512]{1,0:T(8,128)S(1)} %copy-done.1, f32[32,512]{1,0:T(8,128)S(1)} %copy-done.2), kind=kLoop, calls=%fused_computation.2 | loop fusion | flops 196608 | bytes 458752 | tf_op jit(solution)/shard_map/sub | solution.py:45
Async XLA Ops:
  0.6 54.2 %copy-start.2 = (f32[32,512]{1,0:T(8,128)S(1)}, f32[32,512]{1,0:T(8,128)}, u32[]{:S(2)}) copy-start(f32[32,512]{1,0:T(8,128)} %param.17) | copy-start | bytes 196612
  0.6 54.2 %copy-start.1 = (f32[32,512]{1,0:T(8,128)S(1)}, f32[32,512]{1,0:T(8,128)}, u32[]{:S(2)}) copy-start(f32[32,512]{1,0:T(8,128)} %param.16) | copy-start | bytes 196612
  0.7 54.2 %copy-start = (f32[32,512]{1,0:T(8,128)S(1)}, f32[32,512]{1,0:T(8,128)}, u32[]{:S(2)}) copy-start(f32[32,512]{1,0:T(8,128)} %param.15) | copy-start | bytes 196612

commit v6 on v5

--- a/solution.py
+++ b/solution.py
@@ -457,17 +457,18 @@
                 part = nn(onehot_near[s, g], recv_near[s, c, g])
                 acc[table] = part if s == 0 else acc[table] + part
         if c == 0:
-            send_rows(1, SHORT)
             zf_send(chunks)
         else:
             x_send(chunks + c)
         x_send(c)
-    send_rows(1, chunks - 1)
+    send_rows(1, SHORT)
     for s in range(micro):
         for i, block in enumerate(owner_rows(s, slots, lab_recv)):
             onehot[s, :, i * 128 : (i + 1) * 128] = block
     for s in range(micro - 1):
         for c in range(SHORT, chunks):
+            if c == last:
+                send_rows(1, last)
             y_copy(s, c).wait_recv()
             part = nn(onehot[s], recv_y[s, c])
             acc[c] = part if s == 0 else acc[c] + part
@@ -583,7 +584,7 @@
             dma((chunks + 2, max(nz - 1, 1))),
             dma((chunks + 2, max(nz - 1, 1))),
         ],
-        compiler_params=pltpu.CompilerParams(collective_id=0, has_side_effects=True, vmem_limit_bytes=56 * 1024 * 1024),
+        compiler_params=pltpu.CompilerParams(collective_id=0, has_side_effects=True, vmem_limit_bytes=55040 * 1024),
         name="layer_rows",
     )(tokens, cotangent, lengths, item_rows, w_in, w_out)
     return adam_rows(clipped, table, moment_one, moment_two)

time: 56.8 us -> 57.7 us (1.016)
  local copies, waits for them, and re-layouts: 0.01 us -> 1.34 us
  other arithmetic: 1.53 us -> 0.69 us
  Pallas kernels: 54.2 us -> 54.8 us
    unnamed x6 -> x10, local copies, waits for them, and re-layouts: 0.01 us -> 1.34 us
    sub x1, other arithmetic: 1.53 us -> 0.69 us  [adam_rows(): table - step_size * first_moment / scaled]
    pallas_call x1, Pallas kernels: 54.2 us -> 54.8 us  [on_device(): pl.pallas_call(functools.partial(kernel, dims), out_shape=jax.ShapeDtypeS...]
where the time goes in v6:
time: 57.7 us; the launch traced here: 57.5 us
  Pallas kernels  54.8 us (95%)
  local copies, waits for them, and re-layouts  1.34 us (2%)
  other arithmetic  0.69 us (1%)
  between operations  0.68 us (1%)
    pallas_call x1, Pallas kernels, on_device(): pl.pallas_call(functools.partial(kernel, dims), out_shape=jax.ShapeDtypeS...  54.8 us
    unnamed x10, local copies, waits for them, and re-layouts  1.34 us

profile of v6, /device:TPU:1, one launch (start us, length us, event | category | flops | bytes accessed | tf_op | source)
XLA Modules:
  0.0 57.5 jit_solution(8184232508689827583)
XLA Ops:
  0.6 0.0 copy-start
  0.6 0.7 %copy-done = s32[2,256]{1,0:T(2,128)S(1)} copy-done((s32[2,256]{1,0:T(2,128)S(1)}, s32[2,256]{1,0:T(2,128)}, u32[]{:S(2)}) %copy-start) | copy-done | bytes 2072
  1.3 0.0 copy-start.1
  1.3 0.7 %copy-done.1 = s32[2]{0:T(128)S(1)} copy-done((s32[2]{0:T(128)S(1)}, s32[2]{0:T(128)}, u32[]{:S(2)}) %copy-start.1) | copy-done | bytes 32
  2.0 0.0 copy-start.2
  2.0 0.0 copy-start.3
  2.0 0.0 copy-start.4
  2.0 54.8 %layer_rows.1 = f32[32,512]{1,0:T(8,128)S(1)} custom-call(bf16[2,256,512]{2,1,0:T(8,128)(2,1)} %tokens_hbm.1, bf16[2,256,512]{2,1,0:T(8,128)(2,1)} %cot_hbm.1, s32[2]{0:T(128)S(1)} %copy-done.1, s32[2,256]{1,0:T(2,128)S(1)} %copy-done, bf16[512,2048]{1,0:T(8,128)(2,1)} %w_in_hbm.1, bf16[512,512]{1,0:T(8,128)(2,1)} %w_out_hbm.1), custom_call_target="tpu_custom_call" | custom-call | tf_op jit(solution)/shard_map/layer_rows/pallas_call | solution.py:531
  56.8 0.0 copy-done.2
  56.8 0.0 copy-done.3
  56.8 0.0 copy-done.4
  56.8 0.7 %divide_subtract_fusion = (f32[32,512]{1,0:T(8,128)}, f32[32,512]{1,0:T(8,128)}, f32[32,512]{1,0:T(8,128)}) fusion(f32[32,512]{1,0:T(8,128)S(1)} %copy-done.2, f32[32,512]{1,0:T(8,128)S(1)} %layer_rows.1, f32[32,512]{1,0:T(8,128)S(1)} %copy-done.3, f32[32,512]{1,0:T(8,128)S(1)} %copy-done.4), kind=kLoop, calls=%fused_computation.2 | loop fusion | flops 196608 | bytes 458752 | tf_op jit(solution)/shard_map/sub | solution.py:45
Async XLA Ops:
  0.6 0.7 %copy-start = (s32[2,256]{1,0:T(2,128)S(1)}, s32[2,256]{1,0:T(2,128)}, u32[]{:S(2)}) copy-start(s32[2,256]{1,0:T(2,128)} %items_hbm.1) | copy-start | bytes 6148
  1.3 0.7 %copy-start.1 = (s32[2]{0:T(128)S(1)}, s32[2]{0:T(128)}, u32[]{:S(2)}) copy-start(s32[2]{0:T(128)} %lengths.1) | copy-start | bytes 28
  2.0 54.8 %copy-start.2 = (f32[32,512]{1,0:T(8,128)S(1)}, f32[32,512]{1,0:T(8,128)}, u32[]{:S(2)}) copy-start(f32[32,512]{1,0:T(8,128)} %param.15) | copy-start | bytes 196612
  2.0 54.8 %copy-start.3 = (f32[32,512]{1,0:T(8,128)S(1)}, f32[32,512]{1,0:T(8,128)}, u32[]{:S(2)}) copy-start(f32[32,512]{1,0:T(8,128)} %param.16) | copy-start | bytes 196612
  2.0 54.8 %copy-start.4 = (f32[32,512]{1,0:T(8,128)S(1)}, f32[32,512]{1,0:T(8,128)}, u32[]{:S(2)}) copy-start(f32[32,512]{1,0:T(8,128)} %param.17) | copy-start | bytes 196612
